TPU v7x, 256 devices: a whole 4x4x8 slice. The times are simulated.
256 devices in a mesh: lon: 8 (over y, x_lo), lat: 16 (over z, x_hi), rep: 2 (over core).
Axes of the slice: x: 4 (x_hi: 2, x_lo: 2; x = x_hi * 2 + x_lo), y: 4, z: 8, core: 2. Of those that a mesh axis runs over, the one named last changes fastest.
Arguments:
- forcing: float32 [8, 4, 2, 512, 2048], P('rep', None, None, 'lat', 'lon'), may hold values from -6 to 6
- diffusivity: float32 [512, 2048], P('lat', 'lon'), may hold values from 0.1 to 0.22
- ocean: int32 [512, 2048], P('lat', 'lon'), may hold values 0 or 1
- phase: float32 [4], replicated, may hold values from 0.1 to 0.4
- site_cell: int32 [16, 8, 2048], P('lat', 'lon'), may hold values from 0 to 8191
- site_count: int32 [16, 8], P('lat', 'lon'), may hold values from 1 to 2048, 10240 in all within a row
- site_weight: float32 [16, 8, 2048], P('lat', 'lon'), may hold values from 0.5 to 5
Outputs:
- representer: float32 [8, 4, 2, 512, 2048], P('rep', None, None, 'lat', 'lon')
- gram: float32 [8, 8], P('rep')
Inputs may be any that keep to these rules, and one draw needn't show every extreme that they name: `site_count`: live slots are the first ones of a block; in each latitude row of blocks one block has all 2048 slots live.
All inputs are finite; a program needn't handle non-finite values. No bound on the sum of `ocean` on one device may be relied on, other than what follows from the above.
Results may differ from a plain program's by a relative error of at most 0.00007.
Values sent between devices are 32-bit elements; how exact they have to be, the bound alone decides.
A program may use at most 64 MiB of HBM per device.

v0:
```python
import jax
import jax.numpy as jnp
from jax import lax
from jax.sharding import Mesh
from jax.sharding import PartitionSpec as P

CONST = 4
SWEEPS = 4
LAT = ("lat_0", "lat_1")
LON_LAT = ("lon_0", "lon_1", "lat_0", "lat_1")
LON = ("lon_0", "lon_1")


DAMPING = 0.9


def padded_2(shard, sides, width):
    for axis, dim in sides:
        devices, length = (lax.axis_size(axis), shard.shape[dim])
        up = [(i, (i + 1) % devices) for i in range(devices)]
        down = [(j, i) for i, j in up]
        last = lax.slice_in_dim(shard, length - width, length, axis=dim)
        leading = lax.slice_in_dim(shard, 0, width, axis=dim)
        before = lax.ppermute(last, axis, up)
        after = lax.ppermute(leading, axis, down)
        shard = jnp.concatenate([before, shard, after], axis=dim)
    return shard


def copy_for_each(shard, axis):
    copies = jnp.broadcast_to(shard, (lax.axis_size(axis), *shard.shape))
    return lax.all_to_all(copies, axis, split_axis=0, concat_axis=0, tiled=True)


def laid_out(pieces, dim):
    pieces = jnp.moveaxis(pieces, 0, dim)
    dims = pieces.shape
    return pieces.reshape(*dims[:dim], dims[dim] * dims[dim + 1], *dims[dim + 2 :])


def gather_directly(shard, axis, dim):
    pieces = copy_for_each(shard, axis)
    return laid_out(pieces, dim)


def one_axis_at_a_time(shard, axes):
    for axis in axes:
        shard = lax.psum(shard, axis)
    return shard


def laplace(padded):
    center = padded[..., 1:-1, 1:-1]
    total = (
        padded[..., 2:, 1:-1]
        + padded[..., :-2, 1:-1]
        + padded[..., 1:-1, 2:]
        + padded[..., 1:-1, :-2]
    )
    return total - 4.0 * center


def rotate(field, cosine, sinus):
    real_part = field[:, :, 0]
    imag_part = field[:, :, 1]
    new_real = cosine * real_part - sinus * imag_part
    new_imag = sinus * real_part + cosine * imag_part
    return jnp.stack([new_real, new_imag], axis=2)


def lat_valid(rows_lat, width):
    first = lax.axis_index(LAT) * rows_lat - width
    latitude = first + jnp.arange(rows_lat + 2 * width, dtype=jnp.int32)
    inside = (latitude >= 0) & (latitude < rows_lat * lax.axis_size(LAT))
    return inside.astype(jnp.float32)[:, None]


def local(forcing, diffusivity, ocean, phase, site_cell, site_count, site_weight):
    rows_lat = forcing.shape[3]
    cols_lon = forcing.shape[4]
    wet = ocean.astype(jnp.float32)
    cosine = jnp.cos(phase)[:, None, None]
    sinus = jnp.sin(phase)[:, None, None]
    depth = SWEEPS
    deep_valid = lat_valid(rows_lat, depth)
    coefficients = jnp.stack([diffusivity, wet], axis=0)
    extended = padded_2(coefficients, ((LON, 2), (LAT, 1)), depth) * deep_valid
    diffuse_ext = extended[0]
    wet_ext = extended[1]

    def window(array, width):
        start = depth - width
        return array[start : start + rows_lat + 2 * width, start : start + cols_lon + 2 * width]

    current = padded_2(forcing, ((LON, 4), (LAT, 3)), depth) * deep_valid
    for step in range(SWEEPS):
        width = depth - step
        product = window(diffuse_ext, width) * current
        inner = current[..., 1:-1, 1:-1]
        current = window(wet_ext, width - 1) * (
            DAMPING * rotate(inner, cosine, -sinus) + laplace(product)
        )
    current = padded_2(current, ((LON, 4), (LAT, 3)), depth) * deep_valid
    for step in range(SWEEPS):
        width = depth - step
        inner = current[..., 1:-1, 1:-1]
        current = window(wet_ext, width - 1) * (
            DAMPING * rotate(inner, cosine, sinus)
            + window(diffuse_ext, width - 1) * laplace(current)
        )
    rep_local = current.shape[0]
    slot_total = site_cell.shape[2]
    flat = current.reshape(rep_local, CONST * 2, rows_lat * cols_lon)
    samples = jnp.take(flat, site_cell[0, 0], axis=2)
    slots = jnp.arange(slot_total, dtype=jnp.int32)
    weight = site_weight[0, 0] * (slots < site_count[0, 0]).astype(jnp.float32)
    weighted = (samples * weight[None, None, :]).reshape(rep_local, -1)
    plain = samples.reshape(rep_local, -1)
    gathered = gather_directly(plain, "rep", 0)
    partial_rows = jnp.dot(
        weighted, gathered.T, precision=lax.Precision.HIGHEST, preferred_element_type=jnp.float32
    )
    scale = float(lax.axis_size(LAT) * lax.axis_size(LON) * slot_total)
    gram = one_axis_at_a_time(partial_rows, LON_LAT) / scale
    return (current, gram)


def solution(mesh):
    torus = Mesh(
        mesh.devices.reshape(4, 2, 8, 2, mesh.shape["rep"]),
        ("lon_0", "lon_1", "lat_0", "lat_1", "rep"),
    )
    return jax.shard_map(
        local,
        mesh=torus,
        in_specs=(
            P("rep", None, None, LAT, LON),
            P(LAT, LON),
            P(LAT, LON),
            P(),
            P(LAT, LON, None),
            P(LAT, LON),
            P(LAT, LON, None),
        ),
        out_specs=(P("rep", None, None, LAT, LON), P("rep", None)),
        check_vma=False,
    )
```

profile of v0, /device:TPU:2, one launch (start us, length us, event | category | flops | bytes accessed | tf_op | source)
XLA Modules:
  0.0 189.4 jit_solution(609035854693240836)
XLA Ops:
  6.1 2.2 %collective-permute-start.4 = (f32[4,4,2,32,4]{4,3,2,1,0:T(8,128)S(1)}, f32[4,4,2,32,4]{4,3,2,1,0:T(8,128)S(1)}, u32[]{:S(2)}, u32[]{:S(2)}) collective-permute-start(f32[4,4,2,32,4]{4,3,2,1,0:T(8,128)S(1)} %get-tuple-element.32), channel_id=1, source_target_pairs={{0,32},{32,64},{64,96},{96,128},{128,160},{160,192},{192,224},{224... | collective-permute-start | bytes 49160 | tf_op jit(solution)/shard_map/ppermute | solution.py:24
  12.0 5.4 %collective-permute-start.3 = (f32[2,4,264]{2,1,0:T(4,128)S(1)}, f32[2,4,264]{2,1,0:T(4,128)S(1)}, u32[]{:S(2)}, u32[]{:S(2)}) collective-permute-start(f32[2,4,264]{2,1,0:T(4,128)S(1)} %get-tuple-element.35), channel_id=1, source_target_pairs={{2,0},{4,2},{6,4},{8,6},{10,8},{12,10},{14,12},{16,14},{18,16},{20... | collective-permute-start | bytes 25352 | tf_op jit(solution)/shard_map/ppermute | solution.py:25
  17.4 13.3 %collective-permute-done.2 = f32[2,4,264]{2,1,0:T(4,128)S(1)} collective-permute-done((f32[2,4,264]{2,1,0:T(4,128)S(1)}, f32[2,4,264]{2,1,0:T(4,128)S(1)}, u32[]{:S(2)}, u32[]{:S(2)}) %collective-permute-start.2) | collective-permute-done | bytes 8480 | tf_op jit(solution)/shard_map/ppermute | solution.py:24
  30.7 2.9 %collective-permute-done.3 = f32[2,4,264]{2,1,0:T(4,128)S(1)} collective-permute-done((f32[2,4,264]{2,1,0:T(4,128)S(1)}, f32[2,4,264]{2,1,0:T(4,128)S(1)}, u32[]{:S(2)}, u32[]{:S(2)}) %collective-permute-start.3) | collective-permute-done | bytes 8480 | tf_op jit(solution)/shard_map/ppermute | solution.py:25
  35.3 5.6 %collective-permute-start.7 = (f32[4,4,2,4,264]{4,3,2,1,0:T(4,128)S(1)}, f32[4,4,2,4,264]{4,3,2,1,0:T(4,128)S(1)}, u32[]{:S(2)}, u32[]{:S(2)}) collective-permute-start(f32[4,4,2,4,264]{4,3,2,1,0:T(4,128)S(1)} %get-tuple-element.13), channel_id=1, source_target_pairs={{2,0},{4,2},{6,4},{8,6},{10,8},{12,10},{14,12},{16,14},{18,16},{20... | collective-permute-start | bytes 405512 | tf_op jit(solution)/shard_map/ppermute | solution.py:25
  41.4 2.8 %collective-permute-done.6 = f32[4,4,2,4,264]{4,3,2,1,0:T(4,128)S(1)} collective-permute-done((f32[4,4,2,4,264]{4,3,2,1,0:T(4,128)S(1)}, f32[4,4,2,4,264]{4,3,2,1,0:T(4,128)S(1)}, u32[]{:S(2)}, u32[]{:S(2)}) %collective-permute-start.6) | collective-permute-done | bytes 135200 | tf_op jit(solution)/shard_map/ppermute | solution.py:24
  47.8 2.1 %broadcast_multiply_fusion.2 = (f32[4,4,2,38,262]{4,3,2,1,0:T(8,128)S(1)}, f32[4,4,2,38,262]{4,3,2,1,0:T(8,128)S(1)}) fusion(f32[38,262]{1,0:T(8,128)S(1)} %slice.362, f32[4,4,2,40,264]{4,3,2,1,0:T(8,128)S(1)} %get-tuple-element.8, f32[4,4,1,38,262]{4,3,2,1,0:T(8,128)S(1)} %get-tuple-element.29, f32[4,4,1,38,262]{4,3,2,1,0:T(8,128)S(1)} %get-tuple-element.28, ...), kind=kLoop, calls=%fused_computation.81 | loop fusion | flops 3185920 | bytes 10274592 | tf_op jit(solution)/shard_map/mul | solution.py:98
  53.4 2.1 %broadcast_multiply_fusion = (f32[4,4,2,34,258]{4,3,2,1,0:T(8,128)S(1)}, f32[4,4,2,34,258]{4,3,2,1,0:T(8,128)S(1)}) fusion(f32[34,258]{1,0:T(8,128)S(1)} %slice.378, f32[4,4,2,36,260]{4,3,2,1,0:T(8,128)S(1)} %get-tuple-element.4, f32[4,4,1,34,258]{4,3,2,1,0:T(8,128)S(1)} %get-tuple-element.25, f32[4,4,1,34,258]{4,3,2,1,0:T(8,128)S(1)} %get-tuple-element.24, ...), kind=kLoop, calls=%fused_computation.77 | loop fusion | flops 2807040 | bytes 9052704 | tf_op jit(solution)/shard_map/mul | solution.py:98
  57.3 2.1 %collective-permute-start.8 = (f32[4,4,2,32,4]{4,3,2,1,0:T(8,128)S(1)}, f32[4,4,2,32,4]{4,3,2,1,0:T(8,128)S(1)}, u32[]{:S(2)}, u32[]{:S(2)}) collective-permute-start(f32[4,4,2,32,4]{4,3,2,1,0:T(8,128)S(1)} %get-tuple-element.30), channel_id=1, source_target_pairs={{0,32},{32,64},{64,96},{96,128},{128,160},{160,192},{192,224},{224... | collective-permute-start | bytes 49160 | tf_op jit(solution)/shard_map/ppermute | solution.py:24
  59.5 12.7 %collective-permute-done.8 = f32[4,4,2,32,4]{4,3,2,1,0:T(8,128)S(1)} collective-permute-done((f32[4,4,2,32,4]{4,3,2,1,0:T(8,128)S(1)}, f32[4,4,2,32,4]{4,3,2,1,0:T(8,128)S(1)}, u32[]{:S(2)}, u32[]{:S(2)}) %collective-permute-start.8) | collective-permute-done | bytes 16416 | tf_op jit(solution)/shard_map/ppermute | solution.py:24
  72.2 11.3 %collective-permute-done.9 = f32[4,4,2,32,4]{4,3,2,1,0:T(8,128)S(1)} collective-permute-done((f32[4,4,2,32,4]{4,3,2,1,0:T(8,128)S(1)}, f32[4,4,2,32,4]{4,3,2,1,0:T(8,128)S(1)}, u32[]{:S(2)}, u32[]{:S(2)}) %collective-permute-start.9) | collective-permute-done | bytes 16416 | tf_op jit(solution)/shard_map/ppermute | solution.py:25
  84.0 5.6 %collective-permute-start.11 = (f32[4,4,2,4,264]{4,3,2,1,0:T(4,128)S(1)}, f32[4,4,2,4,264]{4,3,2,1,0:T(4,128)S(1)}, u32[]{:S(2)}, u32[]{:S(2)}) collective-permute-start(f32[4,4,2,4,264]{4,3,2,1,0:T(4,128)S(1)} %get-tuple-element.11), channel_id=1, source_target_pairs={{2,0},{4,2},{6,4},{8,6},{10,8},{12,10},{14,12},{16,14},{18,16},{20... | collective-permute-start | bytes 405512 | tf_op jit(solution)/shard_map/ppermute | solution.py:25
  89.7 3.7 %collective-permute-done.10 = f32[4,4,2,4,264]{4,3,2,1,0:T(4,128)S(1)} collective-permute-done((f32[4,4,2,4,264]{4,3,2,1,0:T(4,128)S(1)}, f32[4,4,2,4,264]{4,3,2,1,0:T(4,128)S(1)}, u32[]{:S(2)}, u32[]{:S(2)}) %collective-permute-start.10) | collective-permute-done | bytes 135200 | tf_op jit(solution)/shard_map/ppermute | solution.py:24
  95.7 2.2 %fusion.11 = f32[4,4,2,38,262]{4,3,2,1,0:T(8,128)S(1)} fusion(f32[4,4,2,40,264]{4,3,2,1,0:T(8,128)S(1)} %maximum_multiply_fusion.4, f32[4,4,1,38,262]{4,3,2,1,0:T(8,128)S(1)} %get-tuple-element.21, f32[4,4,1,38,262]{4,3,2,1,0:T(8,128)S(1)} %get-tuple-element.20, f32[38,262]{1,0:T(8,128)S(1)} %slice.362, f32[38,262]{1,0:T(8,128)S(1)} %slice.351), kind=kLoop, calls=%fused_computation.21 | loop fusion | flops 3185920 | bytes 9000224 | tf_op jit(solution)/shard_map/mul | solution.py:107
  98.5 2.2 %fusion.7 = f32[4,4,2,36,260]{4,3,2,1,0:T(8,128)S(1)} fusion(f32[4,4,2,38,262]{4,3,2,1,0:T(8,128)S(1)} %fusion.11, f32[4,4,1,36,260]{4,3,2,1,0:T(8,128)S(1)} %get-tuple-element.19, f32[4,4,1,36,260]{4,3,2,1,0:T(8,128)S(1)} %get-tuple-element.18, f32[36,260]{1,0:T(8,128)S(1)} %slice.370, f32[36,260]{1,0:T(8,128)S(1)} %slice.350), kind=kLoop, calls=%fused_computation.13 | loop fusion | flops 2995200 | bytes 8461440 | tf_op jit(solution)/shard_map/mul | solution.py:107
  101.3 2.2 %fusion.3 = f32[4,4,2,34,258]{4,3,2,1,0:T(8,128)S(1)} fusion(f32[4,4,2,36,260]{4,3,2,1,0:T(8,128)S(1)} %fusion.7, f32[4,4,1,34,258]{4,3,2,1,0:T(8,128)S(1)} %get-tuple-element.17, f32[4,4,1,34,258]{4,3,2,1,0:T(8,128)S(1)} %get-tuple-element.16, f32[34,258]{1,0:T(8,128)S(1)} %slice.378, f32[34,258]{1,0:T(8,128)S(1)} %slice.349), kind=kLoop, calls=%fused_computation.5 | loop fusion | flops 2807040 | bytes 7929888 | tf_op jit(solution)/shard_map/mul | solution.py:107
  105.3 10.9 %copy.13 = f32[4,8,8192]{1,0,2:T(4,128)} copy(f32[4,8,8192]{2,1,0:T(8,128)S(1)} %reshape.141) | data formatting | bytes 2097152 | tf_op jit(solution)/shard_map/reshape | solution.py:113
  116.2 21.1 %gather_fusion = f32[2048,4,8]{2,1,0:T(4,128)} fusion(f32[4,8,8192]{1,0,2:T(4,128)} %copy.13, s32[2048]{0:T(1024)S(1)} %broadcast_clamp_fusion), kind=kCustom, calls=%fused_computation | custom fusion | bytes 532480 | tf_op jit(solution)/shard_map/jit(_take)/gather | solution.py:114
  137.3 3.4 %copy.14 = f32[2048,4,8]{0,2,1:T(8,128)S(1)} copy(f32[2048,4,8]{2,1,0:T(4,128)} %gather_fusion) | data formatting | bytes 524288 | tf_op jit(solution)/shard_map/jit(_take)/gather | solution.py:114
  141.9 3.5 %all-to-all-start = ((f32[2,4,16384]{2,1,0:T(4,128)}), f32[2,4,16384]{2,1,0:T(4,128)S(1)}, u32[]{:S(2)}, u32[]{:S(2)}) async-start(f32[2,4,16384]{2,1,0:T(4,128)} %broadcast_in_dim.23), calls=%async_computation | async-start | bytes 1048576 | tf_op jit(solution)/shard_map/all_to_all | solution.py:32
  148.6 10.6 %psum.28 = f32[4,8]{1,0:T(4,128)S(1)} all-reduce(f32[4,8]{1,0:T(4,128)S(1)} %fusion.37), channel_id=1, replica_groups=mesh['lon_0'=4,'lon_1'=2,'lat_0'=8,'lat_1'=2,'rep'=2] {'lon_0'}, use_global_device_ids=true, to_apply=%region_0.1 | all-reduce | flops 32 | bytes 256 | tf_op jit(solution)/shard_map/psum | solution.py:48
  159.2 4.9 %psum.29 = f32[4,8]{1,0:T(4,128)S(1)} all-reduce(f32[4,8]{1,0:T(4,128)S(1)} %psum.28), channel_id=1, replica_groups=mesh['lon_0'=4,'lon_1'=2,'lat_0'=8,'lat_1'=2,'rep'=2] {'lon_1'}, use_global_device_ids=true, to_apply=%region_1.2 | all-reduce | flops 32 | bytes 256 | tf_op jit(solution)/shard_map/psum | solution.py:48
  164.1 18.3 %psum.30 = f32[4,8]{1,0:T(4,128)S(1)} all-reduce(f32[4,8]{1,0:T(4,128)S(1)} %psum.29), channel_id=1, replica_groups=mesh['lon_0'=4,'lon_1'=2,'lat_0'=8,'lat_1'=2,'rep'=2] {'lat_0'}, use_global_device_ids=true, to_apply=%region_2.3 | all-reduce | flops 32 | bytes 256 | tf_op jit(solution)/shard_map/psum | solution.py:48
  182.4 6.4 %psum.31 = f32[4,8]{1,0:T(4,128)S(1)} all-reduce(f32[4,8]{1,0:T(4,128)S(1)} %psum.30), channel_id=1, replica_groups=mesh['lon_0'=4,'lon_1'=2,'lat_0'=8,'lat_1'=2,'rep'=2] {'lat_1'}, use_global_device_ids=true, to_apply=%region_3.4 | all-reduce | flops 32 | bytes 256 | tf_op jit(solution)/shard_map/psum | solution.py:48
  (74 shorter events, 30.3 us)
Async XLA Ops:
  0.6 10.5 %copy-start.2 = (f32[32,256]{1,0:T(8,128)S(1)}, f32[32,256]{1,0:T(8,128)}, u32[]{:S(2)}) copy-start(f32[32,256]{1,0:T(8,128)} %param.8) | copy-start | bytes 98308
  0.6 33.1 %copy-start = (f32[4,4,2,32,256]{4,3,2,1,0:T(8,128)S(1)}, f32[4,4,2,32,256]{4,3,2,1,0:T(8,128)}, u32[]{:S(2)}) copy-start(f32[4,4,2,32,256]{4,3,2,1,0:T(8,128)} %param.7) | copy-start | bytes 3145732
  0.7 9.7 %copy-start.3 = (s32[1,1,2048]{2,1,0:T(1,128)S(1)}, s32[1,1,2048]{2,1,0:T(1,128)}, u32[]{:S(2)}) copy-start(s32[1,1,2048]{2,1,0:T(1,128)} %param.11) | copy-start | bytes 24580
  0.7 10.3 %copy-start.4 = (f32[1,1,2048]{2,1,0:T(1,128)S(1)}, f32[1,1,2048]{2,1,0:T(1,128)}, u32[]{:S(2)}) copy-start(f32[1,1,2048]{2,1,0:T(1,128)} %param.13) | copy-start | bytes 24580
  0.7 10.3 %copy-start.5 = (f32[4]{0:T(128)S(1)}, f32[4]{0:T(128)}, u32[]{:S(2)}) copy-start(f32[4]{0:T(128)} %param.10) | copy-start | bytes 52
  2.3 8.7 %collective-permute-start = (f32[2,32,4]{2,1,0:T(8,128)S(1)}, f32[2,32,4]{2,1,0:T(8,128)S(1)}, u32[]{:S(2)}, u32[]{:S(2)}) collective-permute-start(f32[2,32,4]{2,1,0:T(8,128)S(1)} %get-tuple-element.38), channel_id=1, source_target_pairs={{0,32},{32,64},{64,96},{96,128},{128,160},{160,192},{192,224},{224... | collective-permute-start | bytes 3080 | tf_op jit(solution)/shard_map/ppermute | solution.py:24
  3.9 7.2 %collective-permute-start.1 = (f32[2,32,4]{2,1,0:T(8,128)S(1)}, f32[2,32,4]{2,1,0:T(8,128)S(1)}, u32[]{:S(2)}, u32[]{:S(2)}) collective-permute-start(f32[2,32,4]{2,1,0:T(8,128)S(1)} %get-tuple-element.39), channel_id=1, source_target_pairs={{32,0},{64,32},{96,64},{128,96},{160,128},{192,160},{224,192},{0,2... | collective-permute-start | bytes 3080 | tf_op jit(solution)/shard_map/ppermute | solution.py:25
  6.1 27.6 %collective-permute-start.4 = (f32[4,4,2,32,4]{4,3,2,1,0:T(8,128)S(1)}, f32[4,4,2,32,4]{4,3,2,1,0:T(8,128)S(1)}, u32[]{:S(2)}, u32[]{:S(2)}) collective-permute-start(f32[4,4,2,32,4]{4,3,2,1,0:T(8,128)S(1)} %get-tuple-element.32), channel_id=1, source_target_pairs={{0,32},{32,64},{64,96},{96,128},{128,160},{160,192},{192,224},{224... | collective-permute-start | bytes 49160 | tf_op jit(solution)/shard_map/ppermute | solution.py:24
  8.3 25.4 %collective-permute-start.5 = (f32[4,4,2,32,4]{4,3,2,1,0:T(8,128)S(1)}, f32[4,4,2,32,4]{4,3,2,1,0:T(8,128)S(1)}, u32[]{:S(2)}, u32[]{:S(2)}) collective-permute-start(f32[4,4,2,32,4]{4,3,2,1,0:T(8,128)S(1)} %get-tuple-element.33), channel_id=1, source_target_pairs={{32,0},{64,32},{96,64},{128,96},{160,128},{192,160},{224,192},{0,2... | collective-permute-start | bytes 49160 | tf_op jit(solution)/shard_map/ppermute | solution.py:25
  11.2 19.5 %collective-permute-start.2 = (f32[2,4,264]{2,1,0:T(4,128)S(1)}, f32[2,4,264]{2,1,0:T(4,128)S(1)}, u32[]{:S(2)}, u32[]{:S(2)}) collective-permute-start(f32[2,4,264]{2,1,0:T(4,128)S(1)} %get-tuple-element.34), channel_id=1, source_target_pairs={{0,2},{2,4},{4,6},{6,8},{8,10},{10,12},{12,14},{14,16},{16,18},{18... | collective-permute-start | bytes 25352 | tf_op jit(solution)/shard_map/ppermute | solution.py:24
  12.0 21.6 %collective-permute-start.3 = (f32[2,4,264]{2,1,0:T(4,128)S(1)}, f32[2,4,264]{2,1,0:T(4,128)S(1)}, u32[]{:S(2)}, u32[]{:S(2)}) collective-permute-start(f32[2,4,264]{2,1,0:T(4,128)S(1)} %get-tuple-element.35), channel_id=1, source_target_pairs={{2,0},{4,2},{6,4},{8,6},{10,8},{12,10},{14,12},{16,14},{18,16},{20... | collective-permute-start | bytes 25352 | tf_op jit(solution)/shard_map/ppermute | solution.py:25
  34.1 10.1 %collective-permute-start.6 = (f32[4,4,2,4,264]{4,3,2,1,0:T(4,128)S(1)}, f32[4,4,2,4,264]{4,3,2,1,0:T(4,128)S(1)}, u32[]{:S(2)}, u32[]{:S(2)}) collective-permute-start(f32[4,4,2,4,264]{4,3,2,1,0:T(4,128)S(1)} %get-tuple-element.12), channel_id=1, source_target_pairs={{0,2},{2,4},{4,6},{6,8},{8,10},{10,12},{12,14},{14,16},{16,18},{18... | collective-permute-start | bytes 405512 | tf_op jit(solution)/shard_map/ppermute | solution.py:24
  35.3 10.9 %collective-permute-start.7 = (f32[4,4,2,4,264]{4,3,2,1,0:T(4,128)S(1)}, f32[4,4,2,4,264]{4,3,2,1,0:T(4,128)S(1)}, u32[]{:S(2)}, u32[]{:S(2)}) collective-permute-start(f32[4,4,2,4,264]{4,3,2,1,0:T(4,128)S(1)} %get-tuple-element.13), channel_id=1, source_target_pairs={{2,0},{4,2},{6,4},{8,6},{10,8},{12,10},{14,12},{16,14},{18,16},{20... | collective-permute-start | bytes 405512 | tf_op jit(solution)/shard_map/ppermute | solution.py:25
  57.3 14.9 %collective-permute-start.8 = (f32[4,4,2,32,4]{4,3,2,1,0:T(8,128)S(1)}, f32[4,4,2,32,4]{4,3,2,1,0:T(8,128)S(1)}, u32[]{:S(2)}, u32[]{:S(2)}) collective-permute-start(f32[4,4,2,32,4]{4,3,2,1,0:T(8,128)S(1)} %get-tuple-element.30), channel_id=1, source_target_pairs={{0,32},{32,64},{64,96},{96,128},{128,160},{160,192},{192,224},{224... | collective-permute-start | bytes 49160 | tf_op jit(solution)/shard_map/ppermute | solution.py:24
  59.5 24.0 %collective-permute-start.9 = (f32[4,4,2,32,4]{4,3,2,1,0:T(8,128)S(1)}, f32[4,4,2,32,4]{4,3,2,1,0:T(8,128)S(1)}, u32[]{:S(2)}, u32[]{:S(2)}) collective-permute-start(f32[4,4,2,32,4]{4,3,2,1,0:T(8,128)S(1)} %get-tuple-element.31), channel_id=1, source_target_pairs={{32,0},{64,32},{96,64},{128,96},{160,128},{192,160},{224,192},{0,2... | collective-permute-start | bytes 49160 | tf_op jit(solution)/shard_map/ppermute | solution.py:25
  83.9 9.5 %collective-permute-start.10 = (f32[4,4,2,4,264]{4,3,2,1,0:T(4,128)S(1)}, f32[4,4,2,4,264]{4,3,2,1,0:T(4,128)S(1)}, u32[]{:S(2)}, u32[]{:S(2)}) collective-permute-start(f32[4,4,2,4,264]{4,3,2,1,0:T(4,128)S(1)} %get-tuple-element.10), channel_id=1, source_target_pairs={{0,2},{2,4},{4,6},{6,8},{8,10},{10,12},{12,14},{14,16},{16,18},{18... | collective-permute-start | bytes 405512 | tf_op jit(solution)/shard_map/ppermute | solution.py:24
  84.0 10.2 %collective-permute-start.11 = (f32[4,4,2,4,264]{4,3,2,1,0:T(4,128)S(1)}, f32[4,4,2,4,264]{4,3,2,1,0:T(4,128)S(1)}, u32[]{:S(2)}, u32[]{:S(2)}) collective-permute-start(f32[4,4,2,4,264]{4,3,2,1,0:T(4,128)S(1)} %get-tuple-element.11), channel_id=1, source_target_pairs={{2,0},{4,2},{6,4},{8,6},{10,8},{12,10},{14,12},{16,14},{18,16},{20... | collective-permute-start | bytes 405512 | tf_op jit(solution)/shard_map/ppermute | solution.py:25
  105.1 11.1 %copy-start.1 = (f32[4,4,2,32,256]{4,3,2,1,0:T(8,128)}, f32[4,4,2,32,256]{4,3,2,1,0:T(8,128)S(1)}, u32[]{:S(2)}) copy-start(f32[4,4,2,32,256]{4,3,2,1,0:T(8,128)S(1)} %fusion.24) | copy-start | bytes 3145732
  141.9 5.2 %all-to-all-start = ((f32[2,4,16384]{2,1,0:T(4,128)}), f32[2,4,16384]{2,1,0:T(4,128)S(1)}, u32[]{:S(2)}, u32[]{:S(2)}) async-start(f32[2,4,16384]{2,1,0:T(4,128)} %broadcast_in_dim.23), calls=%async_computation | async-start | bytes 1048576 | tf_op jit(solution)/shard_map/all_to_all | solution.py:32
where the time goes:
time: 190 us; the launch traced here: 189 us
  waiting for transfers between devices  51 us (27%)
  blocking collectives  40.3 us (21%)
  local copies, waits for them, and re-layouts  39.4 us (21%)
  starting transfers between devices  30.8 us (16%)
  other arithmetic  25 us (13%)
    psum x4, blocking collectives, one_axis_at_a_time(): shard = lax.psum(shard, axis)  40.3 us
    ppermute x6, waiting for transfers between devices, padded_2(): before = lax.ppermute(last, axis, up)  32.4 us
    gather x2, local copies, waits for them, and re-layouts, local(): samples = jnp.take(flat, site_cell[0, 0], axis=2)  24.5 us
    ppermute x6, starting transfers between devices, padded_2(): after = lax.ppermute(leading, axis, down)  19.3 us
    ppermute x6, waiting for transfers between devices, padded_2(): after = lax.ppermute(leading, axis, down)  17 us
    reshape x2, local copies, waits for them, and re-layouts, local(): flat = current.reshape(rep_local, CONST * 2, rows_lat * cols_lon)  11.1 us
    mul x5, other arithmetic, local(): window(wet_ext, width - 1)  8.83 us
    ppermute x6, starting transfers between devices, padded_2(): before = lax.ppermute(last, axis, up)  7.99 us
  transfers between devices with their start and end apart: 13, of which 9 were waited for; matrix products, arithmetic and copies ran while one was open for 1% of the time, Pallas kernels for 0%

commit v1 on v0

v1 whole, which is shorter than its diff:
```python
import functools

import jax
import jax.numpy as jnp
import numpy as np
from jax import lax
from jax.experimental import pallas as pl
from jax.experimental.pallas import tpu as pltpu
from jax.sharding import PartitionSpec as P

CONST = 4
SWEEPS = 4
DAMPING = 0.9
MESH = pl.DeviceIdType.MESH

DEPTH = 2 * SWEEPS
GROUPS = 2
LANES = 128
OWN_PAIRS = ((0, 0), (1, 1), (0, 1))
CROSS_PAIRS = ((0, 0), (0, 1), (1, 0), (1, 1))


def entry_lanes(rep, row, col):
    a, ra = divmod(row, 2)
    group, local = divmod(col, 4)
    b, rb = divmod(local, 2)
    if group == rep:
        if a > b:
            a, ra, b, rb = b, rb, a, ra
        at = OWN_PAIRS.index((a, b)) * 2 + (ra != rb)
        return [32 * rep + 16 * rb + at]
    first = 6 + CROSS_PAIRS.index((a, b)) * 2 + (ra != rb)
    second = 6 + CROSS_PAIRS.index((b, a)) * 2 + (ra != rb)
    return [32 * rep + 16 * rb + first, 32 * group + 16 * ra + second]


def entry_masks(scale):
    masks = np.zeros((2, 8, 8, LANES), np.float32)
    for rep in range(2):
        for row in range(4):
            for col in range(8):
                for lane in entry_lanes(rep, row, col):
                    masks[rep, col, row, lane] = 1.0 / scale
    return masks


def kernel(
    n_lon,
    n_lat,
    planes_hbm,
    flat_hbm,
    diff_hbm,
    ocean_hbm,
    cell_hbm,
    weight_hbm,
    masks_hbm,
    phase,
    count,
    rep_out,
    gram_out,
    raw,
    out_buf,
    field,
    halo_n,
    halo_s,
    pack,
    east,
    west,
    coef,
    ocean,
    coef_main,
    coef_east,
    coef_west,
    diff_b,
    wet_b,
    trig,
    cell,
    weight,
    masks,
    grid_w,
    partner,
    acc,
    stage1,
    stage2,
    local_sem,
    out_sem,
    lat_send,
    lat_recv,
    lon_send,
    lon_recv,
    corner_send,
    corner_recv,
    coef_send,
    coef_recv,
    part_send,
    part_recv,
    sum1_send,
    sum1_recv,
    sum2_send,
    sum2_recv,
):
    rows, cols = diff_hbm.shape
    i_lon, i_lat, i_rep = lax.axis_index("lon"), lax.axis_index("lat"), lax.axis_index("rep")

    def at(d_lon, d_lat):
        return (
            lax.rem(i_lon + n_lon + d_lon, n_lon),
            lax.rem(i_lat + n_lat + d_lat, n_lat),
            i_rep,
        )

    other = (i_lon, i_lat, 1 - i_rep)
    size1, size2 = n_lat, 2 * n_lon
    i_z, i_half = i_lat // 2, lax.rem(i_lat, 2)
    me1 = i_z * 2 + i_rep
    me2 = i_half * n_lon + i_lon

    def peer1(index):
        return (i_lon, (index // 2) * 2 + i_half, lax.rem(index, 2))

    def peer2(index):
        return (lax.rem(index, n_lon), i_z * 2 + index // n_lon, i_rep)

    neighbours = [(a, b) for a in (-1, 0, 1) for b in (-1, 0, 1) if (a, b) != (0, 0)]

    loads = [
        pltpu.make_async_copy(diff_hbm, coef.at[0], local_sem.at[0]),
        pltpu.make_async_copy(ocean_hbm, ocean, local_sem.at[1]),
        pltpu.make_async_copy(cell_hbm, cell, local_sem.at[2]),
        pltpu.make_async_copy(weight_hbm, weight, local_sem.at[3]),
        pltpu.make_async_copy(masks_hbm, masks, local_sem.at[4]),
    ]
    loads += [
        pltpu.make_async_copy(
            flat_hbm.at[:, pl.ds(t * LANES, LANES)], raw.at[t], local_sem.at[5 + t]
        )
        for t in range(cols // LANES)
    ]
    for load in loads[5:] + loads[:5]:
        load.start()

    barrier = pltpu.get_barrier_semaphore()
    for a, b in neighbours:
        pl.semaphore_signal(barrier, inc=1, device_id=at(a, b), device_id_type=MESH)
    for k in range(1, size1):
        pl.semaphore_signal(
            barrier, inc=1, device_id=peer1(lax.rem(me1 + k, size1)), device_id_type=MESH
        )
    for k in range(1, size2):
        pl.semaphore_signal(
            barrier, inc=1, device_id=peer2(lax.rem(me2 + k, size2)), device_id_type=MESH
        )

    lane = lax.broadcasted_iota(jnp.int32, (8, LANES), 1)
    sub = lax.broadcasted_iota(jnp.int32, (8, LANES), 0)
    angle = jnp.zeros((8, LANES), jnp.float32)
    for c in range(CONST):
        angle = jnp.where(lax.rem(sub, CONST) == c, phase[c], angle)
    trig[0] = DAMPING * jnp.cos(angle)
    trig[1] = DAMPING * jnp.sin(angle)

    loads[0].wait()
    loads[1].wait()
    coef[1] = ocean[...].astype(jnp.float32)
    for load in loads[5:]:
        load.wait()

    def raw_row(ref, rh, p, row, tile):
        start = (16 * rh + p) * rows + row
        return ref[tile, pl.ds(start, 8, stride=2 * rows), :]

    slot = lane // DEPTH
    last = cols // LANES - 1

    def pack_half(index, carry):
        rh, rb = index // 2, lax.rem(index, 2)
        for p in range(2):
            to_west = jnp.zeros((8, LANES), jnp.float32)
            to_east = jnp.zeros((8, LANES), jnp.float32)
            for k in range(16):
                left = raw_row(raw, rh, p, rb * 16 + k, 0)
                right = raw_row(raw, rh, p, rb * 16 + k, last)
                if k:
                    left = pltpu.roll(left, DEPTH * k, 1)
                if k < 15:
                    right = pltpu.roll(right, DEPTH * (k + 1), 1)
                to_west = jnp.where(slot == k, left, to_west)
                to_east = jnp.where(slot == k, right, to_east)
            pack[0, rb, rh, p] = to_west
            pack[1, rb, rh, p] = to_east
        return carry

    lax.fori_loop(0, 4, pack_half, 0)

    pl.semaphore_wait(barrier, len(neighbours) + size1 - 1 + size2 - 1)

    def send(src, dst, sends, recvs, index, device):
        copy = pltpu.make_async_remote_copy(
            src, dst, sends.at[index], recvs.at[index], device_id=device, device_id_type=MESH
        )
        copy.start()
        return copy

    top, low = pl.ds(0, DEPTH), pl.ds(rows - DEPTH, DEPTH)
    body, head, tail = pl.ds(DEPTH, rows), pl.ds(0, DEPTH), pl.ds(rows + DEPTH, DEPTH)
    left_tile, right_tile = pl.ds(0, LANES), pl.ds(cols - LANES, LANES)
    lon_copies = [
        send(pack.at[0], east.at[pl.ds(1, 2)], lon_send, lon_recv, 0, at(-1, 0)),
        send(pack.at[1], west.at[pl.ds(1, 2)], lon_send, lon_recv, 1, at(1, 0)),
    ]
    coef_lon = [
        send(coef.at[:, :, left_tile], coef_east.at[:, body], coef_send, coef_recv, 0, at(-1, 0)),
        send(coef.at[:, :, right_tile], coef_west.at[:, body], coef_send, coef_recv, 1, at(1, 0)),
    ]
    lat_copies = []
    for rh in range(GROUPS):
        pair = []
        for side, (src, dst, hop) in enumerate(((low, halo_n, 1), (top, halo_s, -1))):
            for t in range(cols // LANES):
                pair.append(
                    send(
                        planes_hbm.at[pl.ds(16 * rh, 16), src, pl.ds(t * LANES, LANES)],
                        dst.at[rh, t].reshape(16, DEPTH, LANES),
                        lat_send,
                        lat_recv,
                        4 * rh + 2 * side + t,
                        at(0, hop),
                    )
                )
        lat_copies.append(pair)
    coef_rest = [
        send(coef.at[:, low], coef_main.at[:, head], coef_send, coef_recv, 2, at(0, 1)),
        send(coef.at[:, top], coef_main.at[:, tail], coef_send, coef_recv, 3, at(0, -1)),
        send(
            coef.at[:, low, left_tile], coef_east.at[:, head], coef_send, coef_recv, 4, at(-1, 1)
        ),
        send(
            coef.at[:, top, left_tile], coef_east.at[:, tail], coef_send, coef_recv, 5, at(-1, -1)
        ),
        send(
            coef.at[:, low, right_tile], coef_west.at[:, head], coef_send, coef_recv, 6, at(1, 1)
        ),
        send(
            coef.at[:, top, right_tile], coef_west.at[:, tail], coef_send, coef_recv, 7, at(1, -1)
        ),
    ]
    corner_copies = [
        send(pack.at[0, 1], east.at[0], corner_send, corner_recv, 0, at(-1, 1)),
        send(pack.at[0, 0], east.at[3], corner_send, corner_recv, 1, at(-1, -1)),
        send(pack.at[1, 1], west.at[0], corner_send, corner_recv, 2, at(1, 1)),
        send(pack.at[1, 0], west.at[3], corner_send, corner_recv, 3, at(1, -1)),
    ]

    loads[2].wait()
    loads[3].wait()
    live_slots = count[0, 0]
    row_id = lax.broadcasted_iota(jnp.int32, (rows, LANES), 0)
    col_id = lax.broadcasted_iota(jnp.int32, (cols, LANES), 0)
    lane_1 = lax.broadcasted_iota(jnp.int32, (1, LANES), 1)

    def add_sites(j, total):
        cells = cell[pl.ds(j, 1), :]
        value = jnp.where(j * LANES + lane_1 < live_slots, weight[pl.ds(j, 1), :], 0.0)
        one = value.astype(jnp.bfloat16)
        rest = value - one.astype(jnp.float32)
        two = rest.astype(jnp.bfloat16)
        three = rest - two.astype(jnp.float32)
        hit_row = jnp.broadcast_to(cells // cols, (rows, LANES)) == row_id
        hit_col = jnp.broadcast_to(lax.rem(cells, cols), (cols, LANES)) == col_id
        terms = [
            jnp.where(hit_row, jnp.broadcast_to(term.astype(jnp.float32), (rows, LANES)), 0.0)
            for term in (one, two, three)
        ]
        lhs = jnp.concatenate(terms, axis=0).astype(jnp.bfloat16)
        rhs = jnp.where(hit_col, 1.0, 0.0).astype(jnp.bfloat16)
        return total + lax.dot_general(
            lhs, rhs, (((1,), (1,)), ((), ())), preferred_element_type=jnp.float32
        )

    summed = lax.fori_loop(
        0, cell.shape[0], add_sites, jnp.zeros((3 * rows, cols), jnp.float32)
    )
    summed = summed[:rows] + summed[rows : 2 * rows] + summed[2 * rows :]
    for row in range(rows):
        grid_w[row] = jnp.broadcast_to(summed[row : row + 1], (8, cols))

    def spread(ext, valid):
        for j, dst in enumerate((diff_b, wet_b)):
            far = jnp.where(lane < DEPTH, coef_east[j, pl.ds(ext, 8)], coef_west[j, pl.ds(ext, 8)])
            far = jnp.where((lane < DEPTH) | (lane >= LANES - DEPTH), far, 0.0)
            tiles = [
                coef_main[j, pl.ds(ext, 8), t * LANES : (t + 1) * LANES]
                for t in range(cols // LANES)
            ] + [far]
            for t, tile in enumerate(tiles):
                if valid is not None:
                    tile = jnp.where(valid, tile, 0.0)
                for i in range(8):
                    dst[ext + i, :, t * LANES : (t + 1) * LANES] = jnp.broadcast_to(
                        tile[i : i + 1], (8, LANES)
                    )

    def far_tile(ext, rb, k, rh, p):
        right = east[rb, rh, p]
        left = west[rb, rh, p]
        if k:
            right = pltpu.roll(right, LANES - DEPTH * k, 1)
        if (LANES - DEPTH - DEPTH * k) % LANES:
            left = pltpu.roll(left, LANES - DEPTH - DEPTH * k, 1)
        field[0, rh, p, ext, :, cols : cols + LANES] = jnp.where(lane < LANES // 2, right, left)

    def unpack_body(index, carry):
        rh, rb = index // 2, lax.rem(index, 2)
        for p in range(2):
            for k in range(16):
                row = rb * 16 + k
                for t in range(cols // LANES):
                    field[0, rh, p, DEPTH + row, :, t * LANES : (t + 1) * LANES] = raw_row(
                        raw, rh, p, row, t
                    )
                far_tile(DEPTH + row, rb + 1, k, rh, p)
        return carry

    def unpack_edges(rh):
        for p in range(2):
            for i in range(DEPTH):
                for side, (halo, ext, rb, k) in enumerate(
                    ((halo_n, i, 0, 8 + i), (halo_s, rows + DEPTH + i, 3, i))
                ):
                    for t in range(cols // LANES):
                        at_lanes = slice(t * LANES, (t + 1) * LANES)
                        field[0, rh, p, ext, :, at_lanes] = halo[
                            rh, t, pl.ds(p * DEPTH + i, 8, stride=2 * DEPTH), :
                        ]
                    far_tile(ext, rb, k, rh, p)

    tiles = cols // LANES + 1

    def chunk(src, dst, rh, ext, transposed, final):
        cosine = trig[0]
        sinus = trig[1] if transposed else -trig[1]

        def tile_at(ref, index, t):
            return ref[index + (slice(None), slice(t * LANES, (t + 1) * LANES))]

        value = [
            [[tile_at(field, (src, rh, p, ext + i), t) for t in range(tiles)] for p in range(2)]
            for i in range(-1, 9)
        ]
        if transposed:
            coupling = [
                [tile_at(diff_b, (ext + i,), t) for t in range(tiles)] for i in range(-1, 9)
            ]
            spreads = [
                [[coupling[i][t] * value[i][p][t] for t in range(tiles)] for p in range(2)]
                for i in range(10)
            ]
        else:
            coupling = [None] + [
                [tile_at(diff_b, (ext + i,), t) for t in range(tiles)] for i in range(8)
            ]
            spreads = value
        for i in range(1, 9):
            around = []
            for p in range(2):
                here = spreads[i][p]
                to_right = [pltpu.roll(here[t], 1, 1) for t in range(tiles)]
                to_left = [pltpu.roll(here[t], LANES - 1, 1) for t in range(tiles)]
                total = []
                for t in range(tiles - 1 if final else tiles):
                    w = jnp.where(lane == 0, to_right[(t - 1) % tiles], to_right[t])
                    e = jnp.where(lane == LANES - 1, to_left[(t + 1) % tiles], to_left[t])
                    total.append((spreads[i - 1][p][t] + spreads[i + 1][p][t]) + (e + w))
                around.append(total)
            for t in range(tiles - 1 if final else tiles):
                wet = tile_at(wet_b, (ext + i - 1,), t)
                own = cosine - 4.0 * coupling[i][t]
                real, imag = value[i][0][t], value[i][1][t]
                sums = [around[p][t] for p in range(2)]
                if not transposed:
                    sums = [coupling[i][t] * v for v in sums]
                results = (
                    wet * ((own * real + sinus * imag) + sums[0]),
                    wet * ((own * imag - sinus * real) + sums[1]),
                )
                at_lanes = slice(t * LANES, (t + 1) * LANES)
                for p, result in enumerate(results):
                    field[dst, rh, p, ext + i - 1, :, at_lanes] = result
                    if final:
                        start = (16 * rh + p) * rows + (ext + i - 1 - DEPTH)
                        out_buf[t, pl.ds(start, 8, stride=2 * rows), :] = result

    def interior(step, transposed, final):
        chunks = (rows - 2 * step + 7) // 8

        def one(index, carry):
            rh, k = index // chunks, lax.rem(index, chunks)
            start = jnp.minimum(step + 8 * k, rows - 8 - step)
            chunk(lax.rem(step + 1, 2), lax.rem(step, 2), rh, DEPTH + start, transposed, final)
            return carry

        lax.fori_loop(0, GROUPS * chunks, one, 0)

    def edges(step, rh, transposed, final):
        src, dst = lax.rem(step + 1, 2), lax.rem(step, 2)
        chunk(src, dst, rh, step, transposed, final)
        chunk(src, dst, rh, rows + DEPTH - step, transposed, final)

    def loop(first, stop, body):
        def one(step, carry):
            body(step)
            return carry

        lax.fori_loop(first, stop, one, 0)

    coef_main[:, body] = coef[...]
    for copy in coef_lon:
        copy.wait_recv()
    for ext in range(DEPTH, DEPTH + rows, 8):
        spread(ext, None)
    for copy in lon_copies:
        copy.wait_recv()
    lax.fori_loop(0, 4, unpack_body, 0)
    loop(1, SWEEPS + 1, lambda step: interior(step, True, False))
    loop(SWEEPS + 1, DEPTH, lambda step: interior(step, False, False))
    interior(DEPTH, False, True)

    def share(rh, first, length, index):
        return send(
            field.at[0, rh, 1 - i_rep, pl.ds(DEPTH + first, length), :, pl.ds(0, cols)],
            partner.at[rh, pl.ds(first, length)],
            part_send,
            part_recv,
            index,
            other,
        )

    def put_rows(first, length, index):
        copies = []
        for t in range(cols // LANES):
            copy = pltpu.make_async_copy(
                out_buf.at[t].reshape(rep_out.shape[0], rows, LANES).at[:, pl.ds(first, length)],
                rep_out.at[:, pl.ds(first, length), pl.ds(t * LANES, LANES)],
                out_sem.at[index * (cols // LANES) + t],
            )
            copy.start()
            copies.append(copy)
        return copies

    stores = put_rows(DEPTH, rows - 2 * DEPTH, 0)
    parts = [share(rh, DEPTH, rows - 2 * DEPTH, rh) for rh in range(GROUPS)]
    acc[...] = jnp.zeros_like(acc)

    def own_rows(first, length):
        def one(row, totals):
            totals = list(totals)
            for p in range(2):
                for t in range(cols // LANES):
                    at_lanes = slice(t * LANES, (t + 1) * LANES)
                    values = [field[0, rh, p, DEPTH + row, :, at_lanes] for rh in range(GROUPS)]
                    scaled = [grid_w[row, :, at_lanes] * v for v in values]
                    turned = [pltpu.roll(v, 4, 0) for v in scaled]
                    for j, (a, b) in enumerate(OWN_PAIRS):
                        totals[2 * j] += scaled[a] * values[b]
                        totals[2 * j + 1] += turned[a] * values[b]
            return tuple(totals)

        totals = lax.fori_loop(first, first + length, one, tuple(acc[j] for j in range(6)))
        for j in range(6):
            acc[j] = totals[j]

    def cross_rows(first, length):
        def one(row, totals):
            totals = list(totals)
            for t in range(cols // LANES):
                at_lanes = slice(t * LANES, (t + 1) * LANES)
                scaled = [
                    grid_w[row, :, at_lanes] * field[0, rh, i_rep, DEPTH + row, :, at_lanes]
                    for rh in range(GROUPS)
                ]
                turned = [pltpu.roll(v, 4, 0) for v in scaled]
                values = [partner[rh, row, :, at_lanes] for rh in range(GROUPS)]
                for j, (a, b) in enumerate(CROSS_PAIRS):
                    totals[2 * j] += scaled[a] * values[b]
                    totals[2 * j + 1] += turned[a] * values[b]
            return tuple(totals)

        totals = lax.fori_loop(first, first + length, one, tuple(acc[6 + j] for j in range(8)))
        for j in range(8):
            acc[6 + j] = totals[j]

    own_rows(DEPTH, rows - 2 * DEPTH)
    for copy in parts:
        copy.wait_recv()
    cross_rows(DEPTH, rows - 2 * DEPTH)

    for copy in coef_rest:
        copy.wait_recv()
    spread(0, i_lat > 0)
    spread(rows + DEPTH, i_lat < n_lat - 1)
    for copy in corner_copies:
        copy.wait_recv()
    late = []
    for rh in range(GROUPS):
        for copy in lat_copies[rh]:
            copy.wait_recv()
        unpack_edges(rh)
        loop(1, SWEEPS + 1, lambda step: edges(step, rh, True, False))
        loop(SWEEPS + 1, DEPTH, lambda step: edges(step, rh, False, False))
        edges(DEPTH, rh, False, True)
        late.append(share(rh, 0, DEPTH, 2 + 2 * rh))
        late.append(share(rh, rows - DEPTH, DEPTH, 3 + 2 * rh))
    stores += put_rows(0, DEPTH, 1)
    stores += put_rows(rows - DEPTH, DEPTH, 2)
    own_rows(0, DEPTH)
    own_rows(rows - DEPTH, DEPTH)
    for copy in late:
        copy.wait_recv()
    cross_rows(0, DEPTH)
    cross_rows(rows - DEPTH, DEPTH)

    packed = jnp.zeros((8, LANES), jnp.float32)
    for j in range(14):
        packed = jnp.where(lane == j, jnp.sum(acc[j], axis=1, keepdims=True), packed)
    packed = packed + pltpu.roll(packed, 7, 0)
    packed = packed + pltpu.roll(packed, 6, 0)
    second = pltpu.roll(pltpu.roll(packed, 4, 0), 16, 1)
    packed = jnp.where(lane < 16, packed, second)
    packed = jnp.where(i_rep == 0, packed, pltpu.roll(packed, 32, 1))

    def sum_over(row, buffer, me, size, peer, sends, recvs):
        buffer[me] = row
        copies = []
        for k in range(1, size):
            target = lax.rem(me + k, size)
            copy = pltpu.make_async_remote_copy(
                buffer.at[me],
                buffer.at[me],
                sends.at[target],
                recvs.at[me],
                device_id=peer(target),
                device_id_type=MESH,
            )
            copy.start()
            copies.append(copy)
        for k in range(1, size):
            source = lax.rem(me + k, size)
            pltpu.make_async_remote_copy(
                buffer.at[source],
                buffer.at[source],
                sends.at[source],
                recvs.at[source],
                device_id=peer(source),
                device_id_type=MESH,
            ).wait_recv()
        total = buffer[0]
        for k in range(1, size):
            total = total + buffer[k]
        return total, copies

    row, sum1 = sum_over(packed[0:1], stage1, me1, size1, peer1, sum1_send, sum1_recv)
    row, sum2 = sum_over(row, stage2, me2, size2, peer2, sum2_send, sum2_recv)

    loads[4].wait()
    row = jnp.broadcast_to(row, (8, LANES))
    result = jnp.zeros((8, LANES), jnp.float32)
    for q in range(8):
        result = jnp.where(
            lane == q, jnp.sum(row * masks[i_rep, q], axis=1, keepdims=True), result
        )
    gram_out[...] = result[0:4, 0:8]

    for copy in lon_copies + coef_lon + coef_rest + corner_copies + parts + late + sum1 + sum2:
        copy.wait_send()
    for pair in lat_copies:
        for copy in pair:
            copy.wait_send()
    for copy in stores:
        copy.wait()


def local(n_lon, n_lat, forcing, diffusivity, ocean, phase, site_cell, site_count, site_weight):
    reps, const, parts, rows, cols = forcing.shape
    planes = reps * const * parts
    slots = site_cell.shape[2]
    masks = jnp.asarray(entry_masks(float(n_lon * n_lat * slots)))
    ext = rows + 2 * DEPTH
    wide = cols + LANES
    any_space = pl.BlockSpec(memory_space=pl.ANY)
    vmem = pl.BlockSpec(memory_space=pltpu.VMEM)
    smem = pl.BlockSpec(memory_space=pltpu.SMEM)
    f32 = jnp.float32
    dma = pltpu.SemaphoreType.DMA
    size1, size2 = n_lat, 2 * n_lon
    representer, gram = pl.pallas_call(
        functools.partial(kernel, n_lon, n_lat),
        out_shape=(
            jax.ShapeDtypeStruct((planes, rows, cols), f32),
            jax.ShapeDtypeStruct((reps, 2 * reps), f32),
        ),
        in_specs=[any_space] * 7 + [smem] * 2,
        out_specs=(any_space, vmem),
        scratch_shapes=[
            pltpu.VMEM((cols // LANES, planes * rows, LANES), f32),
            pltpu.VMEM((cols // LANES, planes * rows, LANES), f32),
            pltpu.VMEM((2, GROUPS, 2, ext, 8, wide), f32),
            pltpu.VMEM((GROUPS, cols // LANES, 16 * DEPTH, LANES), f32),
            pltpu.VMEM((GROUPS, cols // LANES, 16 * DEPTH, LANES), f32),
            pltpu.VMEM((2, 2, GROUPS, 2, 8, LANES), f32),
            pltpu.VMEM((4, GROUPS, 2, 8, LANES), f32),
            pltpu.VMEM((4, GROUPS, 2, 8, LANES), f32),
            pltpu.VMEM((2, rows, cols), f32),
            pltpu.VMEM((rows, cols), jnp.int32),
            pltpu.VMEM((2, ext, cols), f32),
            pltpu.VMEM((2, ext, LANES), f32),
            pltpu.VMEM((2, ext, LANES), f32),
            pltpu.VMEM((ext, 8, wide), f32),
            pltpu.VMEM((ext, 8, wide), f32),
            pltpu.VMEM((2, 8, LANES), f32),
            pltpu.VMEM((slots // LANES, LANES), jnp.int32),
            pltpu.VMEM((slots // LANES, LANES), f32),
            pltpu.VMEM(masks.shape, f32),
            pltpu.VMEM((rows, 8, cols), f32),
            pltpu.VMEM((GROUPS, rows, 8, cols), f32),
            pltpu.VMEM((14, 8, LANES), f32),
            pltpu.VMEM((size1, 1, LANES), f32),
            pltpu.VMEM((size2, 1, LANES), f32),
            dma((5 + cols // LANES,)),
            dma((3 * cols // LANES,)),
            dma((4 * cols // LANES,)),
            dma((4 * cols // LANES,)),
            dma((2,)),
            dma((2,)),
            dma((4,)),
            dma((4,)),
            dma((8,)),
            dma((8,)),
            dma((6,)),
            dma((6,)),
            dma((size1,)),
            dma((size1,)),
            dma((size2,)),
            dma((size2,)),
        ],
        compiler_params=pltpu.CompilerParams(
            collective_id=0, has_side_effects=True, vmem_limit_bytes=48 << 20
        ),
        name="representer_block",
    )(
        forcing.reshape(planes, rows, cols),
        forcing.reshape(planes * rows, cols),
        diffusivity,
        ocean,
        site_cell.reshape(slots // LANES, LANES),
        site_weight.reshape(slots // LANES, LANES),
        masks,
        phase,
        site_count,
    )
    return representer.reshape(forcing.shape), gram


def solution(mesh):
    return jax.shard_map(
        functools.partial(local, mesh.shape["lon"], mesh.shape["lat"]),
        mesh=mesh,
        in_specs=(
            P("rep", None, None, "lat", "lon"),
            P("lat", "lon"),
            P("lat", "lon"),
            P(),
            P("lat", "lon", None),
            P("lat", "lon"),
            P("lat", "lon", None),
        ),
        out_specs=(P("rep", None, None, "lat", "lon"), P("rep", None)),
        check_vma=False,
    )
```

time: 190 us -> 61.4 us (0.32)
  the two profiles are of different devices: /device:TPU:2 before, /device:TPU:1 now
where the time goes in v1:
time: 61.4 us; the launch traced here: 61 us
  Pallas kernels  53.2 us (87%)
  local copies, waits for them, and re-layouts  6.47 us (11%)
  between operations  1.32 us (2%)
    pallas_call x1, Pallas kernels, local(): pl.pallas_call(functools.partial(kernel, n_lon, n_lat), out_shape=(jax.Sh...  53.2 us
    unnamed x16, local copies, waits for them, and re-layouts  6.47 us

profile of v1, /device:TPU:1, one launch (start us, length us, event | category | flops | bytes accessed | tf_op | source)
XLA Modules:
  0.0 61.0 jit_solution(2017240770567356954)
XLA Ops:
  0.6 0.0 copy-start.4
  1.3 0.0 copy-start.6
  1.3 0.0 copy-done.4
  1.3 0.6 %copy-done.6 = f32[4]{0:T(128)S(1)} copy-done((f32[4]{0:T(128)S(1)}, f32[4]{0:T(128)}, u32[]{:S(2)}) %copy-start.6) | copy-done | bytes 40
  2.0 0.0 copy-start
  2.0 1.2 %copy-done = f32[4,4,2,32,256]{4,3,2,1,0:T(8,128)S(1)} copy-done((f32[4,4,2,32,256]{4,3,2,1,0:T(8,128)S(1)}, f32[4,4,2,32,256]{4,3,2,1,0:T(8,128)}, u32[]{:S(2)}) %copy-start) | copy-done | bytes 1048600
  3.2 0.0 copy-start.1
  3.2 0.8 %copy-done.1 = f32[2,8,8,128]{3,2,1,0:T(8,128)S(1)} copy-done((f32[2,8,8,128]{3,2,1,0:T(8,128)S(1)}, f32[2,8,8,128]{3,2,1,0:T(8,128)}, u32[]{:S(2)}) %copy-start.1) | copy-done | bytes 65560
  4.0 0.0 copy-start.2
  4.0 0.8 %copy-done.2 = f32[32,256]{1,0:T(8,128)S(1)} copy-done((f32[32,256]{1,0:T(8,128)S(1)}, f32[32,256]{1,0:T(8,128)}, u32[]{:S(2)}) %copy-start.2) | copy-done | bytes 32792
  4.8 0.0 copy-start.3
  4.8 0.8 %copy-done.3 = s32[32,256]{1,0:T(8,128)S(1)} copy-done((s32[32,256]{1,0:T(8,128)S(1)}, s32[32,256]{1,0:T(8,128)}, u32[]{:S(2)}) %copy-start.3) | copy-done | bytes 32792
  5.5 0.0 copy-start.5
  5.5 0.7 %copy-done.5 = f32[1,1,2048]{2,1,0:T(1,128)S(1)} copy-done((f32[1,1,2048]{2,1,0:T(1,128)S(1)}, f32[1,1,2048]{2,1,0:T(1,128)}, u32[]{:S(2)}) %copy-start.5) | copy-done | bytes 8216
  6.2 53.2 %representer_block.1 = (f32[32,32,256]{2,1,0:T(8,128)S(1)}, f32[4,8]{1,0:T(4,128)S(1)}) custom-call(f32[32,32,256]{2,1,0:T(8,128)S(1)} %bitcast.5, f32[1024,256]{1,0:T(8,128)S(1)} %bitcast.6, f32[32,256]{1,0:T(8,128)S(1)} %copy-done.2, s32[32,256]{1,0:T(8,128)S(1)} %copy-done.3, s32[16,128]{1,0:T(8,128)S(1)} %bitcast.8, f32[16,128]{1,0:T(8,128)S(1)} %bitcast.9, ...), custom_call_target="tpu_custom_call" | custom-call | tf_op jit(solution)/shard_map/representer_block/pallas_call | solution.py:595
  59.5 1.0 %copy.13 = f32[4,4,2,32,256]{4,3,2,1,0:T(8,128)} copy(f32[4,4,2,32,256]{4,3,2,1,0:T(8,128)S(1)} %bitcast.7) | data formatting | bytes 2097152
  60.5 0.6 copy.14
Async XLA Ops:
  0.6 0.7 %copy-start.4 = (s32[1,1,2048]{2,1,0:T(1,128)S(1)}, s32[1,1,2048]{2,1,0:T(1,128)}, u32[]{:S(2)}) copy-start(s32[1,1,2048]{2,1,0:T(1,128)} %param.12) | copy-start | bytes 24580
  1.3 0.7 %copy-start.6 = (f32[4]{0:T(128)S(1)}, f32[4]{0:T(128)}, u32[]{:S(2)}) copy-start(f32[4]{0:T(128)} %phase.1) | copy-start | bytes 52
  2.0 1.2 %copy-start = (f32[4,4,2,32,256]{4,3,2,1,0:T(8,128)S(1)}, f32[4,4,2,32,256]{4,3,2,1,0:T(8,128)}, u32[]{:S(2)}) copy-start(f32[4,4,2,32,256]{4,3,2,1,0:T(8,128)} %param.8) | copy-start | bytes 3145732
  3.2 0.8 %copy-start.1 = (f32[2,8,8,128]{3,2,1,0:T(8,128)S(1)}, f32[2,8,8,128]{3,2,1,0:T(8,128)}, u32[]{:S(2)}) copy-start(f32[2,8,8,128]{3,2,1,0:T(8,128)} %constant.2.clone.masks_hbm) | copy-start | bytes 196612
  4.0 0.8 %copy-start.2 = (f32[32,256]{1,0:T(8,128)S(1)}, f32[32,256]{1,0:T(8,128)}, u32[]{:S(2)}) copy-start(f32[32,256]{1,0:T(8,128)} %diff_hbm.1) | copy-start | bytes 98308
  4.8 0.8 %copy-start.3 = (s32[32,256]{1,0:T(8,128)S(1)}, s32[32,256]{1,0:T(8,128)}, u32[]{:S(2)}) copy-start(s32[32,256]{1,0:T(8,128)} %ocean_hbm.1) | copy-start | bytes 98308
  5.5 0.7 %copy-start.5 = (f32[1,1,2048]{2,1,0:T(1,128)S(1)}, f32[1,1,2048]{2,1,0:T(1,128)}, u32[]{:S(2)}) copy-start(f32[1,1,2048]{2,1,0:T(1,128)} %param.14) | copy-start | bytes 24580

commit v2 on v1

v2 whole, which is shorter than its diff:
```python
import functools

import jax
import jax.numpy as jnp
import numpy as np
from jax import lax
from jax.experimental import pallas as pl
from jax.experimental.pallas import tpu as pltpu
from jax.sharding import PartitionSpec as P

CONST = 4
SWEEPS = 4
DAMPING = 0.9
MESH = pl.DeviceIdType.MESH

DEPTH = 2 * SWEEPS
GROUPS = 2
LANES = 128
OWN_PAIRS = ((0, 0), (1, 1), (0, 1))
CROSS_PAIRS = ((0, 0), (0, 1), (1, 0), (1, 1))


def entry_lanes(rep, row, col):
    a, ra = divmod(row, 2)
    group, local = divmod(col, 4)
    b, rb = divmod(local, 2)
    if group == rep:
        if a > b:
            a, ra, b, rb = b, rb, a, ra
        at = OWN_PAIRS.index((a, b)) * 2 + (ra != rb)
        return [32 * rep + 16 * rb + at]
    first = 6 + CROSS_PAIRS.index((a, b)) * 2 + (ra != rb)
    second = 6 + CROSS_PAIRS.index((b, a)) * 2 + (ra != rb)
    return [32 * rep + 16 * rb + first, 32 * group + 16 * ra + second]


def entry_masks(scale):
    masks = np.zeros((2, 8, 8, LANES), np.float32)
    for rep in range(2):
        for row in range(4):
            for col in range(8):
                for lane in entry_lanes(rep, row, col):
                    masks[rep, col, row, lane] = 1.0 / scale
    return masks


def kernel(
    n_lon,
    n_lat,
    planes_hbm,
    diff_hbm,
    ocean_hbm,
    cell_hbm,
    weight_hbm,
    masks_hbm,
    phase_hbm,
    count_hbm,
    rep_out,
    gram_out,
    start,
    odd,
    even,
    strip_start,
    strip_odd,
    strip_even,
    pack,
    east,
    west,
    coef,
    ocean,
    coef_lat,
    factor,
    trig,
    cell,
    weight,
    masks,
    phase,
    count,
    grid_w,
    partner,
    acc,
    stage1,
    stage2,
    load_sem,
    plane_sem,
    out_sem,
    lat_send,
    lat_recv,
    lon_send,
    lon_recv,
    coef_send,
    coef_recv,
    part_send,
    part_recv,
    sum1_send,
    sum1_recv,
    sum2_send,
    sum2_recv,
):
    rows, cols = diff_hbm.shape
    tiles = cols // LANES
    ext_rows = rows + 2 * DEPTH
    i_lon, i_lat, i_rep = lax.axis_index("lon"), lax.axis_index("lat"), lax.axis_index("rep")

    def at(d_lon, d_lat):
        return (
            lax.rem(i_lon + n_lon + d_lon, n_lon),
            lax.rem(i_lat + n_lat + d_lat, n_lat),
            i_rep,
        )

    other = (i_lon, i_lat, 1 - i_rep)
    size1, size2 = n_lat, 2 * n_lon
    i_z, i_half = i_lat // 2, lax.rem(i_lat, 2)
    me1 = i_z * 2 + i_rep
    me2 = i_half * n_lon + i_lon

    def peer1(index):
        return (i_lon, (index // 2) * 2 + i_half, lax.rem(index, 2))

    def peer2(index):
        return (lax.rem(index, n_lon), i_z * 2 + index // n_lon, i_rep)

    neighbours = [(a, b) for a in (-1, 0, 1) for b in (-1, 0, 1) if (a, b) != (0, 0)]
    barrier = pltpu.get_barrier_semaphore()
    for a, b in neighbours:
        pl.semaphore_signal(barrier, inc=1, device_id=at(a, b), device_id_type=MESH)

    def greet(first, stop, peer, me, size):
        def one(k, carry):
            pl.semaphore_signal(
                barrier, inc=1, device_id=peer(lax.rem(me + k, size)), device_id_type=MESH
            )
            return carry

        lax.fori_loop(first, stop, one, 0)

    loads = [
        pltpu.make_async_copy(src, dst, load_sem.at[k])
        for k, (src, dst) in enumerate(
            (
                (diff_hbm, coef.at[0]),
                (ocean_hbm, ocean),
                (cell_hbm, cell),
                (weight_hbm, weight),
                (masks_hbm, masks),
                (phase_hbm, phase),
                (count_hbm, count),
            )
        )
    ]
    own = pl.ds(DEPTH, rows)
    planes = [
        pltpu.make_async_copy(
            planes_hbm.at[16 * rh + 2 * m + p], start.at[rh, p, own, m], plane_sem.at[rh, p, m]
        )
        for rh in range(GROUPS)
        for p in range(2)
        for m in range(8)
    ]
    for load in loads[:2] + planes + loads[5:] + loads[2:5]:
        load.start()
    greet(1, size1, peer1, me1, size1)
    greet(1, size2, peer2, me2, size2)

    lane = lax.broadcasted_iota(jnp.int32, (8, LANES), 1)
    sub = lax.broadcasted_iota(jnp.int32, (8, LANES), 0)
    loads[5].wait()
    angle = jnp.zeros((8, LANES), jnp.float32)
    for c in range(CONST):
        one = jnp.broadcast_to(phase[0:1, c : c + 1], (8, LANES))
        angle = jnp.where(lax.rem(sub, CONST) == c, one, angle)
    trig[0] = DAMPING * jnp.cos(angle)
    trig[1] = DAMPING * jnp.sin(angle)

    def turn(value, shift):
        shift %= LANES
        return pltpu.roll(value, shift, 1) if shift else value

    def span(t):
        return slice(t * LANES, (t + 1) * LANES)

    def set_factors(ext, t, diffusivity, wet):
        inverse = jnp.where(diffusivity > 0.0, 1.0 / jnp.where(diffusivity > 0.0, diffusivity, 1.0), 0.0)
        coupled = wet * diffusivity
        for i in range(8):
            d, w, v, u = (
                jnp.broadcast_to(x[i : i + 1], (8, LANES))
                for x in (diffusivity, wet, inverse, coupled)
            )
            sinus = w * trig[1]
            factor[0, ext + i, :, span(t)] = w * trig[0] - 4.0 * u
            factor[1, ext + i, :, span(t)] = sinus
            factor[2, ext + i, :, span(t)] = -sinus
            factor[3, ext + i, :, span(t)] = u
            factor[4, ext + i, :, span(t)] = v

    for load in loads[:2]:
        load.wait()
    coef[1] = ocean[...].astype(jnp.float32)
    for load in planes:
        load.wait()

    def prepare(block, carry):
        row = pl.multiple_of(block * 8, 8)
        for t in range(tiles):
            diffusivity = coef[0, pl.ds(row, 8), span(t)]
            for i in range(8):
                d = jnp.broadcast_to(diffusivity[i : i + 1], (8, LANES))
                for rh in range(GROUPS):
                    for p in range(2):
                        index = (rh, p, DEPTH + row + i, slice(None), span(t))
                        start[index] = d * start[index]
        return carry

    lax.fori_loop(0, rows // 8, prepare, 0)

    slot = lane // DEPTH

    def pack_half(rb, carry):
        row = rb * 16
        for g in range(2 * GROUPS + 1):
            to_west = jnp.zeros((8, LANES), jnp.float32)
            to_east = jnp.zeros((8, LANES), jnp.float32)
            for k in range(16 if g < 2 * GROUPS else 4):
                if g < 2 * GROUPS:
                    index = (g // 2, g % 2, DEPTH + row + k, slice(None))
                    left, right = start[index + (span(0),)], start[index + (span(tiles - 1),)]
                else:
                    some = pl.ds(pl.multiple_of(row + 8 * (k % 2), 8), 8)
                    left, right = coef[k // 2, some, span(0)], coef[k // 2, some, span(tiles - 1)]
                to_west = jnp.where(slot == k, turn(left, DEPTH * k), to_west)
                to_east = jnp.where(slot == k, turn(right, DEPTH * (k + 1)), to_east)
            pack[0, rb, g] = to_west
            pack[1, rb, g] = to_east
        return carry

    lax.fori_loop(0, 2, pack_half, 0)

    mains, strips = (start, odd, even), (strip_start, strip_odd, strip_even)

    def sweep(refs, prefix, step, ext, count, widths, offset):
        src = refs[0] if step == 1 else refs[1 + step % 2]
        dst = refs[1 if step % 2 else 2]
        sign = 1 if step <= SWEEPS else 2
        value = [
            [
                [src[(*prefix, p, ext + i, slice(None), span(t))] for t in range(widths)]
                for p in range(2)
            ]
            for i in range(-1, count + 1)
        ]
        for i in range(count):
            around = []
            for p in range(2):
                here = value[i + 1][p]
                right = [pltpu.roll(v, 1, 1) for v in here]
                left = [pltpu.roll(v, LANES - 1, 1) for v in here]
                for t in range(widths):
                    w, e = right[t], left[t]
                    if t > 0:
                        w = jnp.where(lane == 0, right[t - 1], w)
                    if t < widths - 1:
                        e = jnp.where(lane == LANES - 1, left[t + 1], e)
                    around.append((value[i][p][t] + value[i + 2][p][t]) + (w + e))
            for t in range(widths):
                at_row = (ext + i, slice(None), span(t + offset))
                a, s, u = factor[(0, *at_row)], factor[(sign, *at_row)], factor[(3, *at_row)]
                real, imag = value[i + 1][0][t], value[i + 1][1][t]
                results = [
                    (a * real + s * imag) + u * around[t],
                    (a * imag - s * real) + u * around[widths + t],
                ]
                if step == SWEEPS:
                    results = [factor[(4, *at_row)] * v for v in results]
                for p in range(2):
                    dst[(*prefix, p, ext + i, slice(None), span(t))] = results[p]

    def main_rows(rh, step, ext, count):
        sweep(mains, (rh,), step, ext, count, tiles, 0)

    def strip_rows(step, ext, count):
        sweep(strips, (), step, ext, count, 1, tiles)

    def interior(step, size, body):
        chunks = (rows - 2 * step + size - 1) // size

        def one(k, carry):
            body(DEPTH + jnp.minimum(step + size * k, rows - size - step))
            return carry

        lax.fori_loop(0, chunks, one, 0)

    def interior_main(steps):
        for step in steps:

            def both(ext, step=step):
                for rh in range(GROUPS):
                    main_rows(rh, step, ext, 8)

            interior(step, 8, both)

    def main_factors(block, carry):
        row = pl.multiple_of(block * 8, 8)
        for t in range(tiles):
            set_factors(
                DEPTH + row, t, coef[0, pl.ds(row, 8), span(t)], coef[1, pl.ds(row, 8), span(t)]
            )
        return carry

    lax.fori_loop(0, rows // 8, main_factors, 0)

    pl.semaphore_wait(barrier, len(neighbours) + size1 - 1 + size2 - 1)

    def send(src, dst, sends, recvs, index, device):
        copy = pltpu.make_async_remote_copy(
            src, dst, sends.at[index], recvs.at[index], device_id=device, device_id_type=MESH
        )
        copy.start()
        return copy

    first, last = pl.ds(DEPTH, DEPTH), pl.ds(rows, DEPTH)
    head, tail = pl.ds(0, DEPTH), pl.ds(rows + DEPTH, DEPTH)
    lon_copies = [
        send(pack.at[0], east.at[pl.ds(1, 2)], lon_send, lon_recv, 0, at(-1, 0)),
        send(pack.at[1], west.at[pl.ds(1, 2)], lon_send, lon_recv, 1, at(1, 0)),
    ]
    coef_copies = [
        send(coef.at[:, last_rows], coef_lat.at[side], coef_send, coef_recv, side, at(0, hop))
        for side, (last_rows, hop) in enumerate(
            ((pl.ds(rows - DEPTH, DEPTH), 1), (pl.ds(0, DEPTH), -1))
        )
    ]
    lat_copies = []
    for rh in range(GROUPS):
        if rh == 1:
            corner_copies = [
                send(pack.at[0, 1], east.at[0], lon_send, lon_recv, 2, at(-1, 1)),
                send(pack.at[0, 0], east.at[3], lon_send, lon_recv, 3, at(-1, -1)),
                send(pack.at[1, 1], west.at[0], lon_send, lon_recv, 4, at(1, 1)),
                send(pack.at[1, 0], west.at[3], lon_send, lon_recv, 5, at(1, -1)),
            ]
        lat_copies.append(
            [
                send(
                    start.at[rh, p, src],
                    start.at[rh, p, dst],
                    lat_send,
                    lat_recv,
                    4 * rh + 2 * p + side,
                    at(0, hop),
                )
                for p in range(2)
                for side, (src, dst, hop) in enumerate(((last, head, 1), (first, tail, -1)))
            ]
        )

    interior_main(range(1, DEPTH + 1))

    def strip_factors(block, main_of, valid):
        rb, half = (block + 1) // 2, (block + 1) % 2
        built = []
        for j in range(2):
            left, right = main_of(j, 0), main_of(j, tiles - 1)
            at_slot = DEPTH * (2 * j + half)
            value = jnp.where(lane < 48, turn(left, 32), 0.0)
            value = jnp.where(lane < 32, turn(west[rb, 2 * GROUPS], 24 - at_slot), value)
            value = jnp.where(lane < 24, turn(east[rb, 2 * GROUPS], 16 - at_slot), value)
            value = jnp.where(lane < 16, turn(right, 16), value)
            value = jnp.where(lane < 64, value, pltpu.roll(value, 64, 1))
            built.append(value if valid is None else jnp.where(valid, value, 0.0))
        set_factors(block * 8, tiles, *built)

    def strip_row(ext, rb, k, valid):
        for p in range(2):
            value = jnp.zeros((8, LANES), jnp.float32)
            for rh in range(GROUPS):
                base = 64 * rh
                index = (rh, p, ext, slice(None))
                part = jnp.where(lane < base + 48, turn(start[index + (span(0),)], base + 32), 0.0)
                part = jnp.where(
                    lane < base + 32, turn(west[rb, 2 * rh + p], base + 24 - DEPTH * k), part
                )
                part = jnp.where(
                    lane < base + 24, turn(east[rb, 2 * rh + p], base + 16 - DEPTH * k), part
                )
                part = jnp.where(
                    lane < base + 16, turn(start[index + (span(tiles - 1),)], base + 16), part
                )
                value = part if rh == 0 else jnp.where(lane < base, value, part)
            if valid is not None:
                value = jnp.where(valid, value, 0.0)
            strip_start[p, ext] = value

    def strip_body(rb, carry):
        for k in range(16):
            strip_row(DEPTH + rb * 16 + k, rb + 1, k, None)
        return carry

    loads[2].wait()
    loads[3].wait()
    loads[6].wait()
    live_slots = jnp.broadcast_to(count[...], (1, LANES))
    row_id = lax.broadcasted_iota(jnp.int32, (rows, LANES), 0)
    col_id = lax.broadcasted_iota(jnp.int32, (cols, LANES), 0)
    lane_1 = lax.broadcasted_iota(jnp.int32, (1, LANES), 1)

    def add_sites(j, total):
        cells = cell[pl.ds(j, 1), :]
        value = jnp.where(j * LANES + lane_1 < live_slots, weight[pl.ds(j, 1), :], 0.0)
        one = value.astype(jnp.bfloat16)
        rest = value - one.astype(jnp.float32)
        two = rest.astype(jnp.bfloat16)
        three = rest - two.astype(jnp.float32)
        hit_row = jnp.broadcast_to(cells // cols, (rows, LANES)) == row_id
        hit_col = jnp.broadcast_to(lax.rem(cells, cols), (cols, LANES)) == col_id
        terms = [
            jnp.where(hit_row, jnp.broadcast_to(term.astype(jnp.float32), (rows, LANES)), 0.0)
            for term in (one, two, three)
        ]
        lhs = jnp.concatenate(terms, axis=0).astype(jnp.bfloat16)
        rhs = jnp.where(hit_col, 1.0, 0.0).astype(jnp.bfloat16)
        return total + lax.dot_general(
            lhs, rhs, (((1,), (1,)), ((), ())), preferred_element_type=jnp.float32
        )

    summed = lax.fori_loop(
        0, cell.shape[0], add_sites, jnp.zeros((3 * rows, cols), jnp.float32)
    )
    summed = summed[:rows] + summed[rows : 2 * rows] + summed[2 * rows :]
    for row in range(rows):
        grid_w[row] = jnp.broadcast_to(summed[row : row + 1], (8, cols))

    for copy in lon_copies:
        copy.wait_recv()
    for block in range(1, 1 + rows // 8):
        strip_factors(
            block, lambda j, t, block=block: coef[j, pl.ds(8 * block - 8, 8), span(t)], None
        )
    lax.fori_loop(0, 2, strip_body, 0)
    for step in range(1, DEPTH + 1):
        interior(step, 16, lambda ext, step=step: strip_rows(step, ext, 16))

    def merge(first_row, length):
        for ext in range(DEPTH + first_row, DEPTH + first_row + length):
            for p in range(2):
                value = strip_even[p, ext]
                for rh in range(GROUPS):
                    left = even.at[rh, p, ext, :, span(0)]
                    right = even.at[rh, p, ext, :, span(tiles - 1)]
                    pltpu.store(left, turn(value, -32 - 64 * rh), mask=lane < DEPTH)
                    pltpu.store(
                        right, turn(value, LANES - 16 - 64 * rh), mask=lane >= LANES - DEPTH
                    )

    def share(rh, first_row, length, index):
        return send(
            even.at[rh, 1 - i_rep, pl.ds(DEPTH + first_row, length)],
            partner.at[rh, pl.ds(first_row, length)],
            part_send,
            part_recv,
            index,
            other,
        )

    merge(DEPTH, rows - 2 * DEPTH)
    parts = [share(rh, DEPTH, rows - 2 * DEPTH, rh) for rh in range(GROUPS)]

    acc[...] = jnp.zeros_like(acc)

    def own_rows(first_row, length):
        def one(block, totals):
            totals = list(totals)
            for row, p, t in [
                (first_row + 4 * block + i, p, t)
                for i in range(4)
                for p in range(2)
                for t in range(tiles)
            ]:
                values = [
                    even[rh, p, DEPTH + row, :, span(t)] for rh in range(GROUPS)
                ]
                scaled = [grid_w[row, :, span(t)] * v for v in values]
                turned = [pltpu.roll(v, 4, 0) for v in scaled]
                for j, (a, b) in enumerate(OWN_PAIRS):
                    totals[2 * j] += scaled[a] * values[b]
                    totals[2 * j + 1] += turned[a] * values[b]
            return tuple(totals)

        totals = lax.fori_loop(
            0, length // 4, one, tuple(acc[j] for j in range(6))
        )
        for j in range(6):
            acc[j] = totals[j]

    def cross_rows(first_row, length):
        def one(block, totals):
            totals = list(totals)
            for row, t in [
                (first_row + 4 * block + i, t) for i in range(4) for t in range(tiles)
            ]:
                scaled = [
                    grid_w[row, :, span(t)] * even[rh, i_rep, DEPTH + row, :, span(t)]
                    for rh in range(GROUPS)
                ]
                turned = [pltpu.roll(v, 4, 0) for v in scaled]
                values = [partner[rh, row, :, span(t)] for rh in range(GROUPS)]
                for j, (a, b) in enumerate(CROSS_PAIRS):
                    totals[2 * j] += scaled[a] * values[b]
                    totals[2 * j + 1] += turned[a] * values[b]
            return tuple(totals)

        totals = lax.fori_loop(
            0, length // 4, one, tuple(acc[6 + j] for j in range(8))
        )
        for j in range(8):
            acc[6 + j] = totals[j]

    own_rows(DEPTH, rows - 2 * DEPTH)
    for copy in parts:
        copy.wait_recv()
    cross_rows(DEPTH, rows - 2 * DEPTH)

    north_in, south_in = i_lat > 0, i_lat < n_lat - 1
    for copy in coef_copies:
        copy.wait_recv()
    for side, (block, valid) in enumerate(((0, north_in), (ext_rows // 8 - 1, south_in))):
        for t in range(tiles):
            set_factors(
                8 * block,
                t,
                *(jnp.where(valid, coef_lat[side, j, :, span(t)], 0.0) for j in range(2)),
            )
    for copy in corner_copies:
        copy.wait_recv()
    for side, (block, valid) in enumerate(((0, north_in), (ext_rows // 8 - 1, south_in))):
        strip_factors(block, lambda j, t, side=side: coef_lat[side, j, :, span(t)], valid)
    for some in lat_copies:
        for copy in some:
            copy.wait_recv()
    for rh in range(GROUPS):
        for ext, valid in ((DEPTH - 1, north_in), (rows + DEPTH, south_in)):
            for p in range(2):
                start[rh, p, ext] = jnp.where(valid, start[rh, p, ext], 0.0)
    for i in range(DEPTH):
        strip_row(i, 0, DEPTH + i, north_in)
        strip_row(rows + DEPTH + i, 3, i, south_in)
    for step in range(1, DEPTH + 1):
        for ext in (step, rows + DEPTH - step):
            for rh in range(GROUPS):
                main_rows(rh, step, ext, DEPTH)
            strip_rows(step, ext, DEPTH)
    merge(0, DEPTH)
    merge(rows - DEPTH, DEPTH)
    late = []
    for rh in range(GROUPS):
        late.append(share(rh, 0, DEPTH, 2 + 2 * rh))
        late.append(share(rh, rows - DEPTH, DEPTH, 3 + 2 * rh))
    stores = [
        pltpu.make_async_copy(
            even.at[rh, p, own, m], rep_out.at[16 * rh + 2 * m + p], out_sem.at[rh, p, m]
        )
        for rh in range(GROUPS)
        for p in range(2)
        for m in range(8)
    ]
    own_rows(0, DEPTH)
    own_rows(rows - DEPTH, DEPTH)
    for copy in late:
        copy.wait_recv()
    cross_rows(0, DEPTH)
    cross_rows(rows - DEPTH, DEPTH)

    packed = jnp.zeros((8, LANES), jnp.float32)
    for j in range(14):
        packed = jnp.where(lane == j, jnp.sum(acc[j], axis=1, keepdims=True), packed)
    packed = packed + pltpu.roll(packed, 7, 0)
    packed = packed + pltpu.roll(packed, 6, 0)
    second = pltpu.roll(pltpu.roll(packed, 4, 0), 16, 1)
    packed = jnp.where(lane < 16, packed, second)
    packed = jnp.where(i_rep == 0, packed, pltpu.roll(packed, 32, 1))

    def sum_start(row, buffer, me, size, peer, sends, recvs):
        buffer[me] = row
        for k in range(1, size):
            target = lax.rem(me + k, size)
            copy = pltpu.make_async_remote_copy(
                buffer.at[me],
                buffer.at[me],
                sends,
                recvs,
                device_id=peer(target),
                device_id_type=MESH,
            )
            copy.start()

    def sum_end(buffer, me, size, peer, sends, recvs):
        several = buffer.at[pl.ds(0, size - 1)]
        pltpu.make_async_remote_copy(
            several, several, sends, recvs, device_id=peer(me), device_id_type=MESH
        ).wait_recv()
        total = buffer[0]
        for k in range(1, size):
            total = total + buffer[k]
        return total

    def sum_sent(buffer, me, size, peer, sends, recvs):
        several = buffer.at[pl.ds(0, size - 1)]
        pltpu.make_async_remote_copy(
            several, several, sends, recvs, device_id=peer(me), device_id_type=MESH
        ).wait_send()

    first_sum = (stage1, me1, size1, peer1, sum1_send, sum1_recv)
    second_sum = (stage2, me2, size2, peer2, sum2_send, sum2_recv)
    sum_start(packed[0:1], *first_sum)
    for store in stores:
        store.start()
    for copy in lon_copies + coef_copies + corner_copies + parts + late:
        copy.wait_send()
    for some in lat_copies:
        for copy in some:
            copy.wait_send()
    loads[4].wait()
    row = sum_end(*first_sum)
    sum_start(row, *second_sum)
    sum_sent(*first_sum)
    for store in stores:
        store.wait()
    row = sum_end(*second_sum)

    row = jnp.broadcast_to(row, (8, LANES))
    result = jnp.zeros((8, LANES), jnp.float32)
    for q in range(8):
        result = jnp.where(
            lane == q, jnp.sum(row * masks[i_rep, q], axis=1, keepdims=True), result
        )
    gram_out[...] = result[0:4, 0:8]

    sum_sent(*second_sum)


def local(n_lon, n_lat, forcing, diffusivity, ocean, phase, site_cell, site_count, site_weight):
    reps, const, parts, rows, cols = forcing.shape
    planes = reps * const * parts
    slots = site_cell.shape[2]
    masks = jnp.asarray(entry_masks(float(n_lon * n_lat * slots)))
    ext = rows + 2 * DEPTH
    wide = cols + LANES
    any_space = pl.BlockSpec(memory_space=pl.ANY)
    vmem = pl.BlockSpec(memory_space=pltpu.VMEM)
    f32 = jnp.float32
    dma = pltpu.SemaphoreType.DMA
    size1, size2 = n_lat, 2 * n_lon
    representer, gram = pl.pallas_call(
        functools.partial(kernel, n_lon, n_lat),
        out_shape=(
            jax.ShapeDtypeStruct((planes, rows, cols), f32),
            jax.ShapeDtypeStruct((reps, 2 * reps), f32),
        ),
        in_specs=[any_space] * 8,
        out_specs=(any_space, vmem),
        scratch_shapes=[
            *[pltpu.VMEM((GROUPS, 2, ext, 8, cols), f32)] * 3,
            *[pltpu.VMEM((2, ext, 8, LANES), f32)] * 3,
            pltpu.VMEM((2, 2, 2 * GROUPS + 1, 8, LANES), f32),
            pltpu.VMEM((4, 2 * GROUPS + 1, 8, LANES), f32),
            pltpu.VMEM((4, 2 * GROUPS + 1, 8, LANES), f32),
            pltpu.VMEM((2, rows, cols), f32),
            pltpu.VMEM((rows, cols), jnp.int32),
            pltpu.VMEM((2, 2, DEPTH, cols), f32),
            pltpu.VMEM((5, ext, 8, wide), f32),
            pltpu.VMEM((2, 8, LANES), f32),
            pltpu.VMEM((slots // LANES, LANES), jnp.int32),
            pltpu.VMEM((slots // LANES, LANES), f32),
            pltpu.VMEM(masks.shape, f32),
            pltpu.VMEM((1, CONST), f32),
            pltpu.VMEM((1, 1), jnp.int32),
            pltpu.VMEM((rows, 8, cols), f32),
            pltpu.VMEM((GROUPS, rows, 8, cols), f32),
            pltpu.VMEM((14, 8, LANES), f32),
            pltpu.VMEM((size1, 1, LANES), f32),
            pltpu.VMEM((size2, 1, LANES), f32),
            dma((7,)),
            dma((GROUPS, 2, 8)),
            dma((GROUPS, 2, 8)),
            dma((8,)),
            dma((8,)),
            dma((6,)),
            dma((6,)),
            dma((2,)),
            dma((2,)),
            dma((6,)),
            dma((6,)),
            dma,
            dma,
            dma,
            dma,
        ],
        compiler_params=pltpu.CompilerParams(
            collective_id=0, has_side_effects=True, vmem_limit_bytes=67043328
        ),
        name="representer_block",
    )(
        forcing.reshape(planes, rows, cols),
        diffusivity,
        ocean,
        site_cell.reshape(slots // LANES, LANES),
        site_weight.reshape(slots // LANES, LANES),
        masks,
        phase.reshape(1, CONST),
        site_count,
    )
    return representer.reshape(forcing.shape), gram


def solution(mesh):
    return jax.shard_map(
        functools.partial(local, mesh.shape["lon"], mesh.shape["lat"]),
        mesh=mesh,
        in_specs=(
            P("rep", None, None, "lat", "lon"),
            P("lat", "lon"),
            P("lat", "lon"),
            P(),
            P("lat", "lon", None),
            P("lat", "lon"),
            P("lat", "lon", None),
        ),
        out_specs=(P("rep", None, None, "lat", "lon"), P("rep", None)),
        check_vma=False,
    )
```

time: 61.4 us -> 46.4 us (0.76)
  Pallas kernels: 53.2 us -> 42 us
  local copies, waits for them, and re-layouts: 6.47 us -> 2.89 us
    pallas_call x1, Pallas kernels: 53.2 us -> 42 us  [local(): pl.pallas_call(functools.partial(kernel, n_lon, n_lat), out_shape=(jax.Sh...]
    unnamed x16 -> x4, local copies, waits for them, and re-layouts: 6.47 us -> 2.89 us
where the time goes in v2:
time: 46.4 us; the launch traced here: 46.2 us
  Pallas kernels  42 us (91%)
  local copies, waits for them, and re-layouts  2.89 us (6%)
  between operations  1.29 us (3%)
    pallas_call x1, Pallas kernels, local(): pl.pallas_call(functools.partial(kernel, n_lon, n_lat), out_shape=(jax.Sh...  42 us
    unnamed x4, local copies, waits for them, and re-layouts  2.89 us

profile of v2, /device:TPU:1, one launch (start us, length us, event | category | flops | bytes accessed | tf_op | source)
XLA Modules:
  0.0 46.2 jit_solution(8127221905050916753)
XLA Ops:
  1.3 42.0 %representer_block.1 = (f32[32,32,256]{2,1,0:T(8,128)}, f32[4,8]{1,0:T(4,128)}) custom-call(f32[32,32,256]{2,1,0:T(8,128)} %bitcast.5, f32[32,256]{1,0:T(8,128)} %diff_hbm.1, s32[32,256]{1,0:T(8,128)} %ocean_hbm.1, s32[16,128]{1,0:T(8,128)} %bitcast.7, f32[16,128]{1,0:T(8,128)} %bitcast.8, f32[2,8,8,128]{3,2,1,0:T(8,128)} %constant.2.clone.masks_hbm, ...), custom_call_target="tpu_custom_call" | custom-call | tf_op jit(solution)/shard_map/representer_block/pallas_call | solution.py:654
  43.3 0.0 copy-start
  43.3 2.3 %copy.13 = f32[4,4,2,32,256]{4,3,2,1,0:T(8,128)} copy(f32[4,4,2,32,256]{4,3,2,1,0:T(8,128)} %bitcast.6) | data formatting | bytes 2097152
  45.7 0.0 copy-done
  45.7 0.6 %copy.14 = f32[4,8]{1,0:T(4,128)} copy(f32[4,8]{1,0:T(4,128)S(1)} %copy-done) | data formatting | bytes 256
Async XLA Ops:
  43.3 2.3 %copy-start = (f32[4,8]{1,0:T(4,128)S(1)}, f32[4,8]{1,0:T(4,128)}, u32[]{:S(2)}) copy-start(f32[4,8]{1,0:T(4,128)} %get-tuple-element.9) | copy-start | bytes 388

commit v3 on v2

--- a/solution.py
+++ b/solution.py
@@ -81,6 +81,7 @@
     acc,
     stage1,
     stage2,
+    ready,
     load_sem,
     plane_sem,
     out_sem,
@@ -121,19 +122,39 @@
     def peer2(index):
         return (lax.rem(index, n_lon), i_z * 2 + index // n_lon, i_rep)
 
-    neighbours = [(a, b) for a in (-1, 0, 1) for b in (-1, 0, 1) if (a, b) != (0, 0)]
+    def by_distance(length):
+        return sorted(range(length), key=lambda k: -min(k, length - k))
+
+    others1 = [
+        lax.rem(i_z + z, size1 // 2) * 2 + lax.rem(i_rep + c, 2)
+        for z in by_distance(size1 // 2)
+        for c in (1, 0)
+        if (z, c) != (0, 0)
+    ]
+    others2 = [
+        lax.rem(i_half + h, 2) * n_lon + lax.rem(i_lon + l, n_lon)
+        for l in by_distance(n_lon)
+        for h in (1, 0)
+        if (h, l) != (0, 0)
+    ]
+
+    sides = [at(1, 0), at(-1, 0), at(0, 1), at(0, -1)]
+    known = (
+        sides,
+        [at(2, 0), at(-2, 0), at(0, 2), at(0, -2)],
+        [at(0, 4), at(0, -4), at(0, 1), at(0, -1)],
+        [other],
+    )
     barrier = pltpu.get_barrier_semaphore()
-    for a, b in neighbours:
-        pl.semaphore_signal(barrier, inc=1, device_id=at(a, b), device_id_type=MESH)
-
-    def greet(first, stop, peer, me, size):
-        def one(k, carry):
-            pl.semaphore_signal(
-                barrier, inc=1, device_id=peer(lax.rem(me + k, size)), device_id_type=MESH
-            )
-            return carry
-
-        lax.fori_loop(first, stop, one, 0)
+    for device in sides + [other]:
+        pl.semaphore_signal(barrier, inc=1, device_id=device, device_id_type=MESH)
+
+    def tell(level):
+        for device in known[level]:
+            pl.semaphore_signal(ready.at[level], inc=1, device_id=device, device_id_type=MESH)
+
+    def learn(level):
+        pl.semaphore_wait(ready.at[level], len(known[level]))
 
     loads = [
         pltpu.make_async_copy(src, dst, load_sem.at[k])
@@ -160,8 +181,6 @@
     ]
     for load in loads[:2] + planes + loads[5:] + loads[2:5]:
         load.start()
-    greet(1, size1, peer1, me1, size1)
-    greet(1, size2, peer2, me2, size2)
 
     lane = lax.broadcasted_iota(jnp.int32, (8, LANES), 1)
     sub = lax.broadcasted_iota(jnp.int32, (8, LANES), 0)
@@ -310,7 +329,8 @@
 
     lax.fori_loop(0, rows // 8, main_factors, 0)
 
-    pl.semaphore_wait(barrier, len(neighbours) + size1 - 1 + size2 - 1)
+    pl.semaphore_wait(barrier, len(sides) + 1)
+    tell(0)
 
     def send(src, dst, sends, recvs, index, device):
         copy = pltpu.make_async_remote_copy(
@@ -333,13 +353,6 @@
     ]
     lat_copies = []
     for rh in range(GROUPS):
-        if rh == 1:
-            corner_copies = [
-                send(pack.at[0, 1], east.at[0], lon_send, lon_recv, 2, at(-1, 1)),
-                send(pack.at[0, 0], east.at[3], lon_send, lon_recv, 3, at(-1, -1)),
-                send(pack.at[1, 1], west.at[0], lon_send, lon_recv, 4, at(1, 1)),
-                send(pack.at[1, 0], west.at[3], lon_send, lon_recv, 5, at(1, -1)),
-            ]
         lat_copies.append(
             [
                 send(
@@ -355,7 +368,18 @@
             ]
         )
 
-    interior_main(range(1, DEPTH + 1))
+    interior_main(range(1, SWEEPS + 1))
+    learn(0)
+    corner_copies = [
+        send(pack.at[0, 1], east.at[0], lon_send, lon_recv, 2, at(-1, 1)),
+        send(pack.at[0, 0], east.at[3], lon_send, lon_recv, 3, at(-1, -1)),
+        send(pack.at[1, 1], west.at[0], lon_send, lon_recv, 4, at(1, 1)),
+        send(pack.at[1, 0], west.at[3], lon_send, lon_recv, 5, at(1, -1)),
+    ]
+    tell(1)
+    interior_main(range(SWEEPS + 1, DEPTH + 1))
+    learn(1)
+    tell(2)
 
     def strip_factors(block, main_of, valid):
         rb, half = (block + 1) // 2, (block + 1) % 2
@@ -466,6 +490,8 @@
     merge(DEPTH, rows - 2 * DEPTH)
     parts = [share(rh, DEPTH, rows - 2 * DEPTH, rh) for rh in range(GROUPS)]
 
+    learn(2)
+    tell(3)
     acc[...] = jnp.zeros_like(acc)
 
     def own_rows(first_row, length):
@@ -521,6 +547,7 @@
         copy.wait_recv()
     cross_rows(DEPTH, rows - 2 * DEPTH)
 
+    learn(3)
     north_in, south_in = i_lat > 0, i_lat < n_lat - 1
     for copy in coef_copies:
         copy.wait_recv()
@@ -535,21 +562,21 @@
         copy.wait_recv()
     for side, (block, valid) in enumerate(((0, north_in), (ext_rows // 8 - 1, south_in))):
         strip_factors(block, lambda j, t, side=side: coef_lat[side, j, :, span(t)], valid)
-    for some in lat_copies:
-        for copy in some:
+    for rh in range(GROUPS):
+        for copy in lat_copies[rh]:
             copy.wait_recv()
-    for rh in range(GROUPS):
         for ext, valid in ((DEPTH - 1, north_in), (rows + DEPTH, south_in)):
             for p in range(2):
                 start[rh, p, ext] = jnp.where(valid, start[rh, p, ext], 0.0)
-    for i in range(DEPTH):
-        strip_row(i, 0, DEPTH + i, north_in)
-        strip_row(rows + DEPTH + i, 3, i, south_in)
-    for step in range(1, DEPTH + 1):
-        for ext in (step, rows + DEPTH - step):
-            for rh in range(GROUPS):
+        if rh == GROUPS - 1:
+            for i in range(DEPTH):
+                strip_row(i, 0, DEPTH + i, north_in)
+                strip_row(rows + DEPTH + i, 3, i, south_in)
+        for step in range(1, DEPTH + 1):
+            for ext in (step, rows + DEPTH - step):
                 main_rows(rh, step, ext, DEPTH)
-            strip_rows(step, ext, DEPTH)
+                if rh == GROUPS - 1:
+                    strip_rows(step, ext, DEPTH)
     merge(0, DEPTH)
     merge(rows - DEPTH, DEPTH)
     late = []
@@ -580,10 +607,9 @@
     packed = jnp.where(lane < 16, packed, second)
     packed = jnp.where(i_rep == 0, packed, pltpu.roll(packed, 32, 1))
 
-    def sum_start(row, buffer, me, size, peer, sends, recvs):
+    def sum_start(row, buffer, me, size, peer, targets, sends, recvs):
         buffer[me] = row
-        for k in range(1, size):
-            target = lax.rem(me + k, size)
+        for target in targets:
             copy = pltpu.make_async_remote_copy(
                 buffer.at[me],
                 buffer.at[me],
@@ -594,24 +620,24 @@
             )
             copy.start()
 
-    def sum_end(buffer, me, size, peer, sends, recvs):
+    def sum_end(buffer, me, size, peer, targets, sends, recvs):
         several = buffer.at[pl.ds(0, size - 1)]
         pltpu.make_async_remote_copy(
-            several, several, sends, recvs, device_id=peer(me), device_id_type=MESH
+            several, several, sends, recvs, device_id=peer(targets[0]), device_id_type=MESH
         ).wait_recv()
         total = buffer[0]
         for k in range(1, size):
             total = total + buffer[k]
         return total
 
-    def sum_sent(buffer, me, size, peer, sends, recvs):
+    def sum_sent(buffer, me, size, peer, targets, sends, recvs):
         several = buffer.at[pl.ds(0, size - 1)]
         pltpu.make_async_remote_copy(
-            several, several, sends, recvs, device_id=peer(me), device_id_type=MESH
+            several, several, sends, recvs, device_id=peer(targets[0]), device_id_type=MESH
         ).wait_send()
 
-    first_sum = (stage1, me1, size1, peer1, sum1_send, sum1_recv)
-    second_sum = (stage2, me2, size2, peer2, sum2_send, sum2_recv)
+    first_sum = (stage1, me1, size1, peer1, others1, sum1_send, sum1_recv)
+    second_sum = (stage2, me2, size2, peer2, others2, sum2_send, sum2_recv)
     sum_start(packed[0:1], *first_sum)
     for store in stores:
         store.start()
@@ -680,6 +706,7 @@
             pltpu.VMEM((14, 8, LANES), f32),
             pltpu.VMEM((size1, 1, LANES), f32),
             pltpu.VMEM((size2, 1, LANES), f32),
+            pltpu.SemaphoreType.REGULAR((4,)),
             dma((7,)),
             dma((GROUPS, 2, 8)),
             dma((GROUPS, 2, 8)),
@@ -697,17 +724,22 @@
             dma,
         ],
         compiler_params=pltpu.CompilerParams(
-            collective_id=0, has_side_effects=True, vmem_limit_bytes=67043328
+            collective_id=0, has_side_effects=True, vmem_limit_bytes=40 << 20
         ),
         name="representer_block",
     )(
-        forcing.reshape(planes, rows, cols),
-        diffusivity,
-        ocean,
-        site_cell.reshape(slots // LANES, LANES),
-        site_weight.reshape(slots // LANES, LANES),
-        masks,
-        phase.reshape(1, CONST),
+        *[
+            pltpu.with_memory_space_constraint(x, pltpu.HBM)
+            for x in (
+                forcing.reshape(planes, rows, cols),
+                diffusivity,
+                ocean,
+                site_cell.reshape(slots // LANES, LANES),
+                site_weight.reshape(slots // LANES, LANES),
+                masks,
+                phase.reshape(1, CONST),
+            )
+        ],
         site_count,
     )
     return representer.reshape(forcing.shape), gram

time: 46.4 us -> 43.7 us (0.942)
  local copies, waits for them, and re-layouts: 2.89 us -> 1.55 us
  Pallas kernels: 42 us -> 40.7 us
    unnamed x4 -> x2, local copies, waits for them, and re-layouts: 2.89 us -> 1.55 us
    pallas_call x1, Pallas kernels: 42 us -> 40.7 us  [local(): pl.pallas_call(functools.partial(kernel, n_lon, n_lat), out_shape=(jax.Sh...]
where the time goes in v3:
time: 43.7 us; the launch traced here: 43.6 us
  Pallas kernels  40.7 us (93%)
  local copies, waits for them, and re-layouts  1.55 us (4%)
  between operations  1.29 us (3%)
    pallas_call x1, Pallas kernels, local(): pl.pallas_call(functools.partial(kernel, n_lon, n_lat), out_shape=(jax.Sh...  40.7 us
    unnamed x2, local copies, waits for them, and re-layouts  1.55 us

profile of v3, /device:TPU:1, one launch (start us, length us, event | category | flops | bytes accessed | tf_op | source)
XLA Modules:
  0.0 43.6 jit_solution(17117244116427925667)
XLA Ops:
  1.3 40.7 %representer_block.1 = (f32[32,32,256]{2,1,0:T(8,128)S(1)}, f32[4,8]{1,0:T(4,128)S(1)}) custom-call(f32[32,32,256]{2,1,0:T(8,128)} %bitcast.6, f32[32,256]{1,0:T(8,128)} %diff_hbm.1, s32[32,256]{1,0:T(8,128)} %ocean_hbm.1, s32[16,128]{1,0:T(8,128)} %bitcast.7, f32[16,128]{1,0:T(8,128)} %bitcast.8, f32[2,8,8,128]{3,2,1,0:T(8,128)} %constant.2.clone.masks_hbm, ...), custom_call_target="tpu_custom_call" | custom-call | tf_op jit(solution)/shard_map/representer_block/pallas_call | solution.py:680
  42.0 1.0 %copy.13 = f32[4,4,2,32,256]{4,3,2,1,0:T(8,128)} copy(f32[4,4,2,32,256]{4,3,2,1,0:T(8,128)S(1)} %bitcast.5) | data formatting | bytes 2097152
  43.0 0.6 %copy.14 = f32[4,8]{1,0:T(4,128)} copy(f32[4,8]{1,0:T(4,128)S(1)} %get-tuple-element.9) | data formatting | bytes 256

commit v4 on v3

--- a/solution.py
+++ b/solution.py
@@ -179,7 +179,7 @@
         for p in range(2)
         for m in range(8)
     ]
-    for load in loads[:2] + planes + loads[5:] + loads[2:5]:
+    for load in planes + loads[:2] + loads[5:] + loads[2:5]:
         load.start()
 
     lane = lax.broadcasted_iota(jnp.int32, (8, LANES), 1)
@@ -246,7 +246,7 @@
                     index = (g // 2, g % 2, DEPTH + row + k, slice(None))
                     left, right = start[index + (span(0),)], start[index + (span(tiles - 1),)]
                 else:
-                    some = pl.ds(pl.multiple_of(row + 8 * (k % 2), 8), 8)
+                    some = pl.ds(row + 8 * (k % 2), 8)
                     left, right = coef[k // 2, some, span(0)], coef[k // 2, some, span(tiles - 1)]
                 to_west = jnp.where(slot == k, turn(left, DEPTH * k), to_west)
                 to_east = jnp.where(slot == k, turn(right, DEPTH * (k + 1)), to_east)
@@ -254,7 +254,8 @@
             pack[1, rb, g] = to_east
         return carry
 
-    lax.fori_loop(0, 2, pack_half, 0)
+    for rb in range(2):
+        pack_half(rb, 0)
 
     mains, strips = (start, odd, even), (strip_start, strip_odd, strip_even)
 
@@ -327,7 +328,6 @@
             )
         return carry
 
-    lax.fori_loop(0, rows // 8, main_factors, 0)
 
     pl.semaphore_wait(barrier, len(sides) + 1)
     tell(0)
@@ -368,6 +368,7 @@
             ]
         )
 
+    lax.fori_loop(0, rows // 8, main_factors, 0)
     interior_main(range(1, SWEEPS + 1))
     learn(0)
     corner_copies = [

time: 43.7 us -> 43.7 us (level)
  no operation moved by 1% of the time
where the time goes in v4:
time: 43.7 us; the launch traced here: 43.5 us
  Pallas kernels  40.7 us (93%)
  local copies, waits for them, and re-layouts  1.55 us (4%)
  between operations  1.29 us (3%)
    pallas_call x1, Pallas kernels, local(): pl.pallas_call(functools.partial(kernel, n_lon, n_lat), out_shape=(jax.Sh...  40.7 us
    unnamed x2, local copies, waits for them, and re-layouts  1.55 us

profile of v4, /device:TPU:1, one launch (start us, length us, event | category | flops | bytes accessed | tf_op | source)
XLA Modules:
  0.0 43.5 jit_solution(6207168104271720391)
XLA Ops:
  1.3 40.7 %representer_block.1 = (f32[32,32,256]{2,1,0:T(8,128)S(1)}, f32[4,8]{1,0:T(4,128)S(1)}) custom-call(f32[32,32,256]{2,1,0:T(8,128)} %bitcast.6, f32[32,256]{1,0:T(8,128)} %diff_hbm.1, s32[32,256]{1,0:T(8,128)} %ocean_hbm.1, s32[16,128]{1,0:T(8,128)} %bitcast.7, f32[16,128]{1,0:T(8,128)} %bitcast.8, f32[2,8,8,128]{3,2,1,0:T(8,128)} %constant.2.clone.masks_hbm, ...), custom_call_target="tpu_custom_call" | custom-call | tf_op jit(solution)/shard_map/representer_block/pallas_call | solution.py:681
  42.0 1.0 %copy.13 = f32[4,4,2,32,256]{4,3,2,1,0:T(8,128)} copy(f32[4,4,2,32,256]{4,3,2,1,0:T(8,128)S(1)} %bitcast.5) | data formatting | bytes 2097152
  42.9 0.6 %copy.14 = f32[4,8]{1,0:T(4,128)} copy(f32[4,8]{1,0:T(4,128)S(1)} %get-tuple-element.9) | data formatting | bytes 256
